TPU v7x, 128 devices: a whole 4x4x4 slice. The times are simulated.
128 devices in a mesh: row: 16 (over x, y_lo, core), col: 8 (over z, y_hi).
Axes of the slice: x: 4, y: 4 (y_hi: 2, y_lo: 2; y = y_hi * 2 + y_lo), z: 4, core: 2. Of those that a mesh axis runs over, the one named last changes fastest.
Arguments:
- block_out: bfloat16 [768, 8192], P('row', 'col'), may hold values from -250 to 250
- stream_mid: bfloat16 [768, 8192], P('row', 'col'), may hold values from -250 to 250
- gate_pre: bfloat16 [768, 28672], P('row', 'col'), may hold values from -8 to 8
- up_pre: bfloat16 [768, 28672], P('row', 'col'), may hold values from -6 to 6
- final_gain: float32 [8192], P('col'), may hold values from 0.28 to 1.72
- mlp_gain: float32 [8192], P('col'), may hold values from 0.1 to 1.9
- value_weight: float32 [8192], P('col'), may hold values from -0.006629126 to 0.006629126
- returns: float32 [768], P('row'), may hold values from -6 to 6
- response_mask: int32 [768], P('row'), may hold values from 0 to 1, as said below
- w_gate: bfloat16 [8192, 28672], P('row', 'col'), may hold values from -0.0625 to 0.0625
- w_up: bfloat16 [8192, 28672], P('row', 'col'), may hold values from -0.0625 to 0.0625
- w_down: bfloat16 [28672, 8192], P('col', 'row'), may hold values from -0.03125 to 0.03125
Outputs:
- stream_mid_gradient: bfloat16 [768, 8192], P('row', 'col')
- d_w_down: float32 [28672, 8192], P('col', 'row')
Inputs may be any that keep to these rules, and one draw needn't show every extreme that they name: `response_mask`: the last token of the micro-batch is a response token.
All inputs are finite; a program needn't handle non-finite values.
Results may differ from a plain program's by a relative error of at most 0.0075.
Values may be sent and summed in bfloat16 or wider, within the bound.
A program may use at most 128 MiB of HBM per device.

v0:
```python
import math

import jax
import jax.numpy as jnp
from jax import lax
from jax.sharding import PartitionSpec as P

MODEL_WIDTH = 8192


epsilon = 1e-05


def contract(left, right, left_dim, right_dim):
    return lax.dot_general(
        left, right, (((left_dim,), (right_dim,)), ((), ())), preferred_element_type=jnp.float32
    )


def swiglu_grads(d_hidden, gate_wide, up_wide, sigmoid_gate):
    d_gate = (d_hidden * up_wide * sigmoid_gate * (1.0 + gate_wide * (1.0 - sigmoid_gate))).astype(
        jnp.bfloat16
    )
    d_up = (d_hidden * gate_wide * sigmoid_gate).astype(jnp.bfloat16)
    return (d_gate, d_up)


def local(
    block_out,
    stream_mid,
    gate_pre,
    up_pre,
    final_gain,
    mlp_gain,
    value_weight,
    returns,
    response_mask,
    w_gate,
    w_up,
    w_down,
):
    local_rows = block_out.shape[0]
    total_tokens = local_rows * lax.axis_size("row")
    output_widened = block_out.astype(jnp.float32)
    middle_widened = stream_mid.astype(jnp.float32)
    live = response_mask.astype(jnp.float32)
    value_head = final_gain * value_weight
    count = lax.psum(jnp.sum(live), "row")
    square_out, square_mid, head_sum = lax.psum(
        (
            jnp.sum(output_widened * output_widened, axis=1),
            jnp.sum(middle_widened * middle_widened, axis=1),
            jnp.sum(output_widened * value_head[None, :], axis=1),
        ),
        "col",
    )
    output_inverse_root = lax.rsqrt(square_out / MODEL_WIDTH + epsilon)
    middle_inverse_root = lax.rsqrt(square_mid / MODEL_WIDTH + epsilon)
    value_estimate = output_inverse_root * head_sum
    dvalue = live * (value_estimate - returns) * (total_tokens * math.sqrt(MODEL_WIDTH) / count)
    output_normalized_rows = output_widened * output_inverse_root[:, None]
    adjoint_vector = value_head[None, :] * dvalue[:, None]
    inner_product = lax.psum(jnp.sum(adjoint_vector * output_normalized_rows, axis=1), "col")
    output_gradient = (
        output_inverse_root[:, None]
        * (adjoint_vector - output_normalized_rows * (inner_product / MODEL_WIDTH)[:, None])
    ).astype(jnp.bfloat16)
    full_rows = lax.all_gather(output_gradient, "col", axis=1, tiled=True)
    tiles = lax.all_to_all(full_rows, "row", split_axis=1, concat_axis=0, tiled=True)
    gate_wide = gate_pre.astype(jnp.float32)
    up_wide = up_pre.astype(jnp.float32)
    sigmoid_gate = jax.nn.sigmoid(gate_wide)
    hidden_local = (gate_wide * sigmoid_gate * up_wide).astype(jnp.bfloat16)
    grad_rows = tiles
    d_w_down = contract(lax.all_gather(hidden_local, "row", axis=0, tiled=True), grad_rows, 0, 0)
    grad_rows = tiles
    d_hidden = lax.psum_scatter(
        contract(grad_rows, w_down, 1, 1), "row", scatter_dimension=0, tiled=True
    )
    d_gate, d_up = swiglu_grads(d_hidden, gate_wide, up_wide, sigmoid_gate)
    stacked = jnp.stack([d_gate, d_up])
    piece = lax.all_gather(stacked, "row", axis=1, tiled=True)
    normed_part = contract(piece[0], w_gate, 1, 1) + contract(piece[1], w_up, 1, 1)
    spread = lax.all_to_all(normed_part, "row", split_axis=0, concat_axis=1, tiled=True)
    d_normed = lax.psum_scatter(spread, "col", scatter_dimension=1, tiled=True)
    middle_normalized_rows = middle_widened * middle_inverse_root[:, None]
    scaled_rows = d_normed * mlp_gain[None, :]
    middle_inner_product = lax.psum(jnp.sum(scaled_rows * middle_normalized_rows, axis=1), "col")
    stream_mid_gradient = output_gradient.astype(jnp.float32) + middle_inverse_root[:, None] * (
        scaled_rows - middle_normalized_rows * (middle_inner_product / MODEL_WIDTH)[:, None]
    )
    return (stream_mid_gradient.astype(jnp.bfloat16), d_w_down)


def solution(mesh):
    placed = (
        P("row", "col"),
        P("row", "col"),
        P("row", "col"),
        P("row", "col"),
        P("col"),
        P("col"),
        P("col"),
        P("row"),
        P("row"),
        P("row", "col"),
        P("row", "col"),
        P("col", "row"),
    )
    return jax.shard_map(
        local,
        mesh=mesh,
        in_specs=placed,
        out_specs=(P("row", "col"), P("col", "row")),
        check_vma=False,
    )
```

profile of v0, /device:TPU:2, one launch (start us, length us, event | category | flops | bytes accessed | tf_op | source)
XLA Modules:
  0.0 504.4 jit_solution(10127957731704284936)
XLA Ops:
  7.2 1.3 convert_reduce_fusion
  8.5 24.2 %psum.44 = f32[]{:T(128)} all-reduce(f32[]{:T(128)} %convert_reduce_fusion), channel_id=1, replica_groups=mesh['row'=16,'col'=8] {'row'}, use_global_device_ids=true, to_apply=%region_5.0 | all-reduce | flops 1 | bytes 8 | tf_op jit(solution)/shard_map/psum | solution.py:48
  32.7 0.7 mul.124
  33.4 1.0 fusion.27
  34.4 25.4 %all-reduce.1 = (f32[48]{0:T(128)S(1)}, f32[48]{0:T(128)S(1)}) all-reduce(f32[48]{0:T(128)S(1)} %get-tuple-element.3, f32[48]{0:T(128)S(1)} %get-tuple-element.2), channel_id=1, replica_groups=mesh['row'=16,'col'=8] {'col'}, use_global_device_ids=true, to_apply=%region_3.0 | all-reduce | flops 96 | bytes 768 | tf_op jit(solution)/shard_map/psum | solution.py:49
  60.5 0.7 add_rsqrt_fusion.1
  61.2 1.2 fusion.23
  62.4 19.1 %all-reduce = (f32[48]{0:T(128)S(1)}, f32[48]{0:T(128)S(1)}) all-reduce(f32[48]{0:T(128)S(1)} %get-tuple-element.14, f32[48]{0:T(128)S(1)} %get-tuple-element.13), channel_id=1, replica_groups=mesh['row'=16,'col'=8] {'col'}, use_global_device_ids=true, to_apply=%region_7.0 | all-reduce | flops 96 | bytes 768 | tf_op jit(solution)/shard_map/psum | solution.py:63
  81.5 1.1 fusion.26
  82.6 36.9 %all_gather.9 = bf16[48,8192]{1,0:T(8,128)(2,1)S(1)} all-gather(bf16[48,1024]{1,0:T(8,128)(2,1)S(1)} %fusion.26), channel_id=1, replica_groups=mesh['row'=16,'col'=8] {'col'}, dimensions={1}, use_global_device_ids=true | all-gather | bytes 884736 | tf_op jit(solution)/shard_map/all_gather | solution.py:68
  119.5 0.1 copy.23
  119.6 20.9 %all_to_all.38 = bf16[48,16,512]{2,0,1:T(8,128)(2,1)S(1)} all-to-all(bf16[48,16,512]{2,0,1:T(8,128)(2,1)S(1)} %bitcast.32), channel_id=1, replica_groups=mesh['row'=16,'col'=8] {'row'}, dimensions={1} | all-to-all | bytes 1572864 | tf_op jit(solution)/shard_map/all_to_all | solution.py:69
  140.5 5.7 %fusion.29 = f32[768,3584]{1,0:T(8,128)} fusion(bf16[768,512]{1,0:T(8,128)(2,1)S(1)} %bitcast.34, bf16[3584,512]{1,0:T(8,128)(2,1)S(1)} %copy-done.6), kind=kOutput, calls=%fused_computation.52 | convolution fusion | flops 2818572288 | bytes 15466496 | tf_op jit(solution)/shard_map/dot_general | solution.py:15
  146.2 0.0 all-gather.3.cloned.1.call-start
  146.3 118.7 %reduce-scatter.3.cloned.1.call-done = f32[48,3584]{1,0:T(8,128)} async-done(((f32[768,3584]{1,0:T(8,128)}), f32[48,3584]{1,0:T(8,128)}) %reduce-scatter.3.cloned.1.call-update) | async-done | bytes 688144 | tf_op jit(solution)/shard_map/reduce_scatter | solution.py:77
  265.0 2.3 fusion.14
  267.2 0.9 pad_maximum_fusion
  268.2 0.0 all-gather.5.cloned.1.call-start
  268.2 0.7 all-gather.5.cloned.1.call-update
  269.0 67.3 %all-gather.3.cloned.1.call-done = bf16[2,768,3584]{2,1,0:T(8,128)(2,1)} async-done(((bf16[2,48,3584]{2,1,0:T(8,128)(2,1)}), bf16[2,768,3584]{2,1,0:T(8,128)(2,1)}) %all-gather.3.cloned.1.call-update) | async-done | bytes 11010064 | tf_op jit(solution)/shard_map/all_gather | solution.py:82
  336.2 6.3 %fusion = f32[768,512]{1,0:T(8,128)S(1)} fusion(bf16[512,3584]{1,0:T(8,128)(2,1)} %param.22, bf16[2,768,3584]{2,1,0:T(8,128)(2,1)} %all-gather.3.cloned.1.call-done), kind=kOutput, calls=%fused_computation.1 | convolution fusion | flops 2818572288 | bytes 10747904 | tf_op jit(solution)/shard_map/dot_general | solution.py:15
  342.5 0.5 copy-done.5
  343.0 1.0 copy-done.7
  344.1 3.0 fusion.2
  347.1 38.1 %all_to_all.39 = f32[16,48,512]{2,1,0:T(8,128)S(1)} all-to-all(f32[16,48,512]{2,1,0:T(8,128)S(1)} %bitcast.33), channel_id=1, replica_groups=mesh['row'=16,'col'=8] {'row'}, dimensions={0} | all-to-all | bytes 3145728 | tf_op jit(solution)/shard_map/all_to_all | solution.py:84
  385.2 1.3 copy.21
  386.6 8.3 %all-gather.5.cloned.1.call-done = bf16[768,3584]{1,0:T(8,128)(2,1)} async-done(((bf16[48,3584]{1,0:T(8,128)(2,1)}), bf16[768,3584]{1,0:T(8,128)(2,1)}) %all-gather.5.cloned.1.call-update) | async-done | bytes 5505040 | tf_op jit(solution)/shard_map/all_gather | solution.py:75
  394.9 7.7 %fusion.30 = f32[3584,512]{1,0:T(8,128)} fusion(bf16[768,3584]{1,0:T(8,128)(2,1)} %all-gather.5.cloned.1.call-done, bf16[768,512]{1,0:T(8,128)(2,1)S(1)} %bitcast.35), kind=kOutput, calls=%fused_computation.53 | convolution fusion | flops 2818572288 | bytes 13631488 | tf_op jit(solution)/shard_map/dot_general | solution.py:15
  402.5 71.0 %reduce-scatter.5.cloned.1.call-done = f32[48,1024]{1,0:T(8,128)} async-done(((f32[48,8192]{1,0:T(8,128)}), f32[48,1024]{1,0:T(8,128)}) %reduce-scatter.5.cloned.1.call-update) | async-done | bytes 196624 | tf_op jit(solution)/shard_map/reduce_scatter | solution.py:85
  473.5 1.1 fusion.18
  474.7 21.5 %psum.47 = f32[48]{0:T(128)S(1)} all-reduce(f32[48]{0:T(128)S(1)} %fusion.18), channel_id=1, replica_groups=mesh['row'=16,'col'=8] {'col'}, use_global_device_ids=true, to_apply=%region_13.0 | all-reduce | flops 48 | bytes 384 | tf_op jit(solution)/shard_map/psum | solution.py:88
  496.1 1.7 fusion.22
  (22 shorter events, 0.2 us)
Async XLA Ops:
  7.2 257.8 %reduce-scatter.3.cloned.1.call-start = ((), (), s32[]{:S(2)}) async-start(), calls=%async_computation.4 | async-start | bytes 11698176 | tf_op jit(solution)/shard_map/reduce_scatter | solution.py:77
  81.4 59.0 %copy-start.6 = (bf16[3584,512]{1,0:T(8,128)(2,1)S(1)}, bf16[3584,512]{1,0:T(8,128)(2,1)}, u32[]{:S(2)}) copy-start(bf16[3584,512]{1,0:T(8,128)(2,1)} %param.23) | copy-start | bytes 11010052
  146.2 118.8 %copy-start.2 = (bf16[48,3584]{1,0:T(8,128)(2,1)S(1)}, bf16[48,3584]{1,0:T(8,128)(2,1)}, u32[]{:S(2)}) copy-start(bf16[48,3584]{1,0:T(8,128)(2,1)} %param.14) | copy-start | bytes 1032196
  146.2 118.8 %copy-start.3 = (bf16[48,3584]{1,0:T(8,128)(2,1)S(1)}, bf16[48,3584]{1,0:T(8,128)(2,1)}, u32[]{:S(2)}) copy-start(bf16[48,3584]{1,0:T(8,128)(2,1)} %param.15) | copy-start | bytes 1032196
  146.2 190.0 %all-gather.3.cloned.1.call-start = ((), (), s32[]{:S(2)}) async-start(), calls=%async_computation.5 | async-start | bytes 11698176 | tf_op jit(solution)/shard_map/all_gather | solution.py:82
  268.2 126.7 %all-gather.5.cloned.1.call-start = ((), (), s32[]{:S(2)}) async-start(), calls=%async_computation.7 | async-start | bytes 5849088 | tf_op jit(solution)/shard_map/all_gather | solution.py:75
  268.9 204.6 %reduce-scatter.5.cloned.1.call-start = ((), (), s32[]{:S(2)}) async-start(), calls=%async_computation.6 | async-start | bytes 1769472 | tf_op jit(solution)/shard_map/reduce_scatter | solution.py:85
  336.2 6.8 %copy-start.5 = (bf16[2,768,3584]{2,1,0:T(8,128)(2,1)S(1)}, bf16[2,768,3584]{2,1,0:T(8,128)(2,1)}, u32[]{:S(2)}) copy-start(bf16[2,768,3584]{2,1,0:T(8,128)(2,1)} %all-gather.3.cloned.1.call-done) | copy-start | bytes 33030148
  336.2 7.8 %copy-start.7 = (bf16[512,3584]{1,0:T(8,128)(2,1)S(1)}, bf16[512,3584]{1,0:T(8,128)(2,1)}, u32[]{:S(2)}) copy-start(bf16[512,3584]{1,0:T(8,128)(2,1)} %param.21) | copy-start | bytes 11010052
  386.5 87.0 %copy-start.1 = (bf16[48,1024]{1,0:T(8,128)(2,1)S(1)}, bf16[48,1024]{1,0:T(8,128)(2,1)}, u32[]{:S(2)}) copy-start(bf16[48,1024]{1,0:T(8,128)(2,1)} %param.13) | copy-start | bytes 294916
  386.5 87.0 %copy-start.4 = (f32[1024]{0:T(1024)S(1)}, f32[1024]{0:T(1024)}, u32[]{:S(2)}) copy-start(f32[1024]{0:T(1024)} %param.17) | copy-start | bytes 12292
  386.6 109.6 %copy-start = (bf16[48,1024]{1,0:T(8,128)(2,1)S(1)}, bf16[48,1024]{1,0:T(8,128)(2,1)}, u32[]{:S(2)}) copy-start(bf16[48,1024]{1,0:T(8,128)(2,1)} %param.12) | copy-start | bytes 294916
Sparse Core Ops, SparseCore 0:
  146.3 118.5 reduce-scatter.2
  268.3 67.8 all-gather.2
  337.9 56.8 all-gather.4
  398.4 75.0 reduce-scatter.4
where the time goes:
time: 505 us; the launch traced here: 504 us
  waiting for transfers between devices  266 us (53%)
  blocking collectives  186 us (37%)
  matrix products  22.7 us (4%)
  between operations  14.5 us (3%)
  other arithmetic  12 us (2%)
    reduce_scatter x1, waiting for transfers between devices, local(): lax.psum_scatter(contract(grad_rows, w_down, 1, 1), 'row', scatter_dimens...  119 us
    reduce_scatter x1, waiting for transfers between devices, local(): d_normed = lax.psum_scatter(spread, 'col', scatter_dimension=1, tiled=True)  71 us
    all_gather x1, waiting for transfers between devices, local(): piece = lax.all_gather(stacked, 'row', axis=1, tiled=True)  67.3 us
    all_to_all x1, blocking collectives, local(): lax.all_to_all(normed_part, 'row', split_axis=0, concat_axis=1, tiled=True)  38.1 us
    all_gather x1, blocking collectives, local(): full_rows = lax.all_gather(output_gradient, 'col', axis=1, tiled=True)  36.9 us
    psum x1, blocking collectives, local(): lax.psum((jnp.sum(output_widened * output_widened, axis=1), jnp.sum(middl...  25.4 us
    psum x1, blocking collectives, local(): count = lax.psum(jnp.sum(live), 'row')  24.2 us
    dot_general x4, matrix products, contract(): lax.dot_general(left, right, (((left_dim,), (right_dim,)), ((), ())), pre...  22.7 us
  transfers between devices with their start and end apart: 4, of which 4 were waited for; matrix products, arithmetic and copies ran while one was open for 4% of the time, Pallas kernels for 0%

commit v1 on v0

v1 whole, which is shorter than its diff:
```python
import functools
import math

import jax
import jax.numpy as jnp
from jax import lax
from jax.experimental import pallas as pl
from jax.experimental.pallas import tpu as pltpu
from jax.sharding import PartitionSpec as P

EPSILON = 1e-05
MESH = pl.DeviceIdType.MESH
F32 = jnp.float32
BF16 = jnp.bfloat16


def nt(left, right):
    return lax.dot_general(left, right, (((1,), (1,)), ((), ())), preferred_element_type=F32)


def hint(value, factor):
    return pl.multiple_of(value, factor)


class Sems:
    def __init__(self, ref):
        self.ref, self.used = ref, 0

    def __call__(self):
        self.used += 1
        return self.ref.at[self.used - 1]


N_SEND, N_RECV, N_LOCAL = 96, 96, 24


def kernel(
    block_hbm, mid_hbm, gate_hbm, up_hbm, final_gain, mlp_gain, value_weight, token_hbm, w_gate, w_up, w_down,
    out_hbm, hid, dout_hbm,
    blk, mid, gains, tok, gx, ux, wd, wg, wu, fa, fb, hid_own,
    square, stat, share, tile, head8, head_j, dout, part_sum,
    rf, nl, nr, ha, hb, ml, mr, my, dg, yf, yb, sb, zs, zr, vs, dn, fin, outv,
    send_sems, recv_sems, local_sems, z_sems,
):
    t, width = blk.shape
    half = gx.shape[2]
    feat = width // 2
    tokens = 16 * t
    model = 8 * width
    n_tile = min(256, half)
    f_tile = min(256, feat)
    r, c = lax.axis_index("row"), lax.axis_index("col")
    k, j = lax.rem(r, 2), lax.div(r, 2)
    x, y = lax.div(j, 2), lax.rem(j, 2)
    z, b = lax.div(c, 2), lax.rem(c, 2)
    k1, y1, b1 = 1 - k, 1 - y, 1 - b
    xr, xl, xf = lax.rem(x + 1, 4), lax.rem(x + 3, 4), lax.rem(x + 2, 4)
    zp, zm, zf = lax.rem(z + 1, 4), lax.rem(z + 3, 4), lax.rem(z + 2, 4)
    sibling = (2 * j + k1, c)
    right, left = (4 * xr + 2 * y + k, c), (4 * xl + 2 * y + k, c)
    partner = (4 * x + 2 * y1 + k, c)
    z_plus, z_minus = (r, 2 * zp + b), (r, 2 * zm + b)
    own_half = pl.ds(hint(k * half, 128), half)
    other_half = pl.ds(hint(k1 * half, 128), half)
    diagonal = j == c
    off_diagonal = j != c
    new_send, new_recv, new_local = Sems(send_sems), Sems(recv_sems), Sems(local_sems)
    sent = []

    def send(src, dst, to, recv, when=None):
        copy = pltpu.make_async_remote_copy(
            src_ref=src, dst_ref=dst, send_sem=new_send(), recv_sem=recv, device_id=to, device_id_type=MESH
        )
        if when is None:
            copy.start()
        else:
            pl.when(when)(copy.start)
        sent.append((copy, when))

    def arrived(dst, recv):
        pltpu.make_async_copy(dst, dst, recv).wait()

    def fetch(src, dst):
        copy = pltpu.make_async_copy(src, dst, new_local())
        copy.start()
        return copy

    barrier = pltpu.get_barrier_semaphore()

    def greet(device):
        pl.semaphore_signal(barrier, inc=1, device_id=device, device_id_type=MESH)

    def perm_to(which):
        return (2 * c + k, 2 * x + which)

    def perm_from(which):
        return (2 * (2 * z + which) + k, j)

    for step in range(1, 8):
        greet((r, lax.rem(c + step, 8)))
    for step in range(1, 16):
        greet((lax.rem(r + step, 16), c))
    greet(perm_to(y1))
    greet(perm_from(b1))

    @pl.when(off_diagonal)
    def _():
        greet(perm_to(y))
        greet(perm_from(b))

    small = [
        fetch(block_hbm, blk),
        fetch(mid_hbm, mid),
        fetch(final_gain, gains.at[0]),
        fetch(value_weight, gains.at[1]),
        fetch(mlp_gain, gains.at[2]),
        fetch(token_hbm, tok),
    ]
    halves = [fetch(gate_hbm.at[:, own_half], gx.at[k]), fetch(up_hbm.at[:, own_half], ux.at[k])]
    own_rows = pl.ds(hint(k * feat, 16), feat)
    weights_down = fetch(w_down.at[own_half, :], wd.at[k])
    weights_in = [fetch(w_gate.at[:, own_half], wg.at[own_rows]), fetch(w_up.at[:, own_half], wu.at[own_rows])]
    for copy in small:
        copy.wait()

    lane = lax.broadcasted_iota(jnp.int32, (t, 128), 1)
    head8[...] = jnp.broadcast_to(gains[0] * gains[1], head8.shape)
    block_wide = blk[...].astype(F32)
    mid_wide = mid[...].astype(F32)
    square[...] = jnp.zeros_like(square)
    sum_out = jnp.sum(block_wide * block_wide, axis=1, keepdims=True)
    sum_head = jnp.sum(block_wide * head8[0:1, :], axis=1, keepdims=True)
    sum_mid = jnp.sum(mid_wide * mid_wide, axis=1, keepdims=True)
    square[0:t, :] = jnp.where(
        lane == 0, sum_out, jnp.where(lane == 1, sum_head, jnp.where(lane == 2, sum_mid, 0.0))
    )
    stat[c] = jnp.transpose(square[...])[0:8, :]

    @pl.when(off_diagonal)
    def _():
        pl.semaphore_wait(barrier, 26)

    @pl.when(diagonal)
    def _():
        pl.semaphore_wait(barrier, 24)

    perm_same, perm_other, perm_head = new_recv(), new_recv(), new_recv()
    send(block_hbm, tile.at[k, j], perm_to(y), perm_same, off_diagonal)
    send(block_hbm, tile.at[k, j], perm_to(y1), perm_other)
    send(head8, head_j, perm_to(y), perm_head, off_diagonal)

    @pl.when(diagonal)
    def _():
        tile[k, j] = blk[...]
        head_j[...] = head8[...]

    stat_recv = []
    for step in range(1, 8):
        stat_recv.append(new_recv())
        send(stat.at[c], stat.at[c], (r, lax.rem(c + step, 8)), stat_recv[-1])
    gate_recv, up_recv, wd_recv, wg_recv, wu_recv = (new_recv() for _ in range(5))
    send(gate_hbm.at[:, other_half], gx.at[k], sibling, gate_recv)
    send(up_hbm.at[:, other_half], ux.at[k], sibling, up_recv)
    send(w_down.at[other_half, :], wd.at[k], sibling, wd_recv)

    for copy in halves:
        copy.wait()
    arrived(gx.at[k1], gate_recv)
    arrived(ux.at[k1], up_recv)
    for q in range(2):

        @pl.loop(0, t // 16)
        def _(i):
            rows = pl.ds(hint(i * 16, 16), 16)
            out_rows = pl.ds(hint(q * t + i * 16, 16), 16)
            gate, up = gx[q, rows, :].astype(F32), ux[q, rows, :].astype(F32)
            sig = jax.nn.sigmoid(gate)
            silu = gate * sig
            fa[out_rows, :] = up * sig * (1.0 + gate * (1.0 - sig))
            fb[out_rows, :] = silu
            hid_own[out_rows, :] = (silu * up).astype(BF16)

    for step in range(1, 8):
        arrived(stat.at[lax.rem(c + 8 - step, 8)], stat_recv[step - 1])
    total = stat[0]
    for i in range(1, 8):
        total = total + stat[i]
    inverse_out = lax.rsqrt(total[0:1] / model + EPSILON)
    inverse_mid = lax.rsqrt(total[2:3] / model + EPSILON)
    value = inverse_out * total[1:2]
    live = tok[1:2, :]
    miss = live * (value - tok[0:1, :])
    slope = inverse_out * miss
    row = lax.broadcasted_iota(jnp.int32, (8, 128), 0)
    own_share = pl.ds(hint(8 * r, 8), 8)
    share[own_share, :] = jnp.where(
        row == 0,
        slope,
        jnp.where(
            row == 1,
            -slope * inverse_out * value / model,
            jnp.where(row == 2, live, jnp.where(row == 3, inverse_mid, 0.0)),
        ),
    )
    share_recv = []
    for step in range(1, 16):
        share_recv.append(new_recv())
        send(share.at[own_share], share.at[own_share], (lax.rem(r + step, 16), c), share_recv[-1])

    def hid_slot(slot, rows=None):
        return hid.at[slot, :, own_half] if rows is None else hid.at[slot, pl.ds(rows, t), own_half]

    def hid_sib(slot):
        return hid.at[slot, :, other_half]

    hid_recv = [new_recv() for _ in range(8)]
    hid_sib_recv = [new_recv() for _ in range(8)]
    slot_own, slot_part = 2 * x + y, 2 * x + y1
    slot_l, slot_r, slot_f = 2 * xl + y, 2 * xr + y, 2 * xf + y
    slot_lo, slot_ro, slot_fo = 2 * xl + y1, 2 * xr + y1, 2 * xf + y1

    def pair(zz):
        return tile.at[k, pl.ds(2 * zz, 2)]

    def pair_sib(zz):
        return tile.at[k1, pl.ds(2 * zz, 2)]

    z_left, z_right, z_far_a, z_far_b = (new_recv() for _ in range(4))
    sib_tile = [new_recv() for _ in range(4)]

    @pl.when(off_diagonal)
    def _():
        arrived(tile.at[k, c], perm_same)
        arrived(head_j, perm_head)

    arrived(tile.at[k, 2 * z + b1], perm_other)
    send(pair(z), pair(z), z_plus, z_left)
    send(pair(z), pair(z), z_minus, z_right)
    send(pair(z), pair(z), sibling, sib_tile[0])

    own_hid = fetch(hid_own, hid_slot(slot_own))
    send(hid_own, hid_slot(slot_own), partner, hid_recv[0])
    send(hid_own, hid_slot(slot_own), right, hid_recv[1])
    send(hid_own, hid_slot(slot_own), left, hid_recv[2])
    send(hid_own, hid_slot(slot_own), sibling, hid_sib_recv[0])

    arrived(pair(zm), z_left)
    send(tile.at[k, 2 * zm], tile.at[k, 2 * zm], z_plus, z_far_a)
    send(pair(zm), pair(zm), sibling, sib_tile[1])
    arrived(pair(zp), z_right)
    send(tile.at[k, 2 * zp + 1], tile.at[k, 2 * zp + 1], z_minus, z_far_b)
    send(pair(zp), pair(zp), sibling, sib_tile[2])

    for step in range(1, 16):
        from_row = lax.rem(r + 16 - step, 16)
        arrived(share.at[pl.ds(hint(8 * from_row, 8), 8)], share_recv[step - 1])
    shares = share[...]
    which = lax.rem(lax.broadcasted_iota(jnp.int32, (128, 128), 0), 8)
    count = jnp.sum(jnp.sum(jnp.where(which == 2, shares, 0.0), axis=0, keepdims=True), axis=1, keepdims=True)
    factor = tokens * math.sqrt(model) / count
    columns = jnp.transpose(shares) * factor
    square[0:8, :] = share[own_share, :]
    own_columns = jnp.transpose(square[...])

    arrived(tile.at[k, 2 * zf], z_far_a)
    arrived(tile.at[k, 2 * zf + 1], z_far_b)
    send(pair(zf), pair(zf), sibling, sib_tile[3])
    for where, sem in zip((z, zm, zp, zf), sib_tile):
        arrived(pair_sib(where), sem)

    head_row = head_j[0:1, :]
    for s in range(8):
        for q in range(2):
            at = 8 * (2 * s + q)
            dout[(2 * s + q) * t : (2 * s + q + 1) * t, :] = (
                columns[0:t, at : at + 1] * head_row + columns[0:t, at + 1 : at + 2] * tile[q, s].astype(F32)
            ).astype(BF16)
    dout_copy = fetch(dout.at[:, pl.ds(hint(k * feat, 128), feat)], dout_hbm)
    own_dout = (
        (own_columns[0:t, 0:1] * factor) * head8[0:1, :] + (own_columns[0:t, 1:2] * factor) * blk[...].astype(F32)
    ).astype(BF16)
    outv[...] = own_dout
    inverse_mid_column = own_columns[0:t, 3:4]

    weights_down.wait()
    arrived(wd.at[k1], wd_recv)
    send(w_gate.at[:, other_half], wg.at[own_rows], sibling, wg_recv)
    send(w_up.at[:, other_half], wu.at[own_rows], sibling, wu_recv)

    def chunk(slot, first=0, size=2 * t):
        return part_sum.at[pl.ds(hint(slot * 2 * t + first, 16), size)]

    def hidden_pair(xs):
        rows = pl.ds(hint(xs * 4 * t, 16), 4 * t)

        @pl.loop(0, half // n_tile)
        def _(n):
            units = pl.ds(hint(n * n_tile, 128), n_tile)
            part_sum[rows, units] = (
                nt(dout[rows, 0:feat], wd[0, units, :]) + nt(dout[rows, feat:], wd[1, units, :])
            ).astype(BF16)

    def add_into(slot, other, first=0, size=2 * t):
        @pl.loop(0, size // 16)
        def _(i):
            rows = pl.ds(hint(slot * 2 * t + first + i * 16, 16), 16)
            their = pl.ds(hint(i * 16, 16), 16)
            part_sum[rows, :] = (part_sum[rows, :].astype(F32) + other[their, :].astype(F32)).astype(BF16)

    rf_s, nl_s, nr_s, ha_s, hb_s, ml_s, mr_s, my_s = (new_recv() for _ in range(8))
    hidden_pair(xf)
    send(chunk(slot_fo), rf, partner, rf_s)
    hidden_pair(xr)
    send(chunk(slot_ro), nl, right, nl_s)
    hidden_pair(xl)
    send(chunk(slot_lo), nr, left, nr_s)
    hidden_pair(x)
    arrived(rf, rf_s)
    add_into(slot_f, rf)
    send(chunk(slot_f, 0, t), ha, right, ha_s)
    send(chunk(slot_f, t, t), hb, left, hb_s)
    arrived(nl, nl_s)
    add_into(slot_part, nl)
    arrived(nr, nr_s)
    add_into(slot_part, nr)
    send(chunk(slot_part), my, partner, my_s)
    arrived(ha, ha_s)
    add_into(slot_r, ha, 0, t)
    send(chunk(slot_r), ml, right, ml_s)
    arrived(hb, hb_s)
    add_into(slot_l, hb, t, t)
    send(chunk(slot_l), mr, left, mr_s)
    arrived(my, my_s)
    arrived(ml, ml_s)
    arrived(mr, mr_s)

    @pl.loop(0, 2 * t // 16)
    def _(i):
        rows = pl.ds(hint(i * 16, 16), 16)
        d_hidden = (
            part_sum[pl.ds(hint(slot_own * 2 * t + i * 16, 16), 16), :].astype(F32)
            + ml[rows, :].astype(F32)
            + mr[rows, :].astype(F32)
            + my[rows, :].astype(F32)
        )
        dg[slot_own, 0, rows, :] = (d_hidden * fa[rows, :]).astype(BF16)
        dg[slot_own, 1, rows, :] = (d_hidden * fb[rows, :]).astype(BF16)

    dg_recv = [new_recv() for _ in range(8)]
    sb_recv = [new_recv() for _ in range(8)]
    pending = []
    last = []

    def product(slot):
        @pl.loop(0, width // f_tile)
        def _(n):
            features = pl.ds(hint(n * f_tile, 128), f_tile)
            piece = nt(dg[slot, 0], wg[features, :]) + nt(dg[slot, 1], wu[features, :])
            yf[slot, :, features] = piece
            yb[slot, :, features] = piece.astype(BF16)

        sem = sb_recv[len(last) + len(pending)]
        send(yb.at[slot, pl.ds(hint(k1 * t, 16), t)], sb.at[slot], sibling, sem)
        pending.append((slot, sem))

    def combine():
        slot, sem = pending.pop(0)
        arrived(sb.at[slot], sem)
        zz, bb = lax.div(slot, 2), lax.rem(slot, 2)
        both = (yf[slot, pl.ds(hint(k * t, 16), t), :] + sb[slot].astype(F32)).astype(BF16)
        zs[slot] = both
        send(zs.at[slot], zr.at[bb, z], (r, 2 * zz + b), z_sems.at[bb, z], zz != z)

        @pl.when(zz == z)
        def _():
            zr[bb, z] = both

        last.append(slot)

    def whole(slot):
        return dg.at[slot]

    send(whole(slot_own), whole(slot_own), right, dg_recv[1])
    send(whole(slot_own), whole(slot_own), left, dg_recv[2])
    send(whole(slot_own), whole(slot_own), partner, dg_recv[0])
    for copy in weights_in:
        copy.wait()
    other_rows = pl.ds(hint(k1 * feat, 16), feat)
    arrived(wg.at[other_rows], wg_recv)
    arrived(wu.at[other_rows], wu_recv)
    product(slot_own)
    arrived(whole(slot_l), dg_recv[1])
    send(dg.at[slot_l, 0], dg.at[slot_l, 0], right, dg_recv[3])
    arrived(whole(slot_r), dg_recv[2])
    send(dg.at[slot_r, 1], dg.at[slot_r, 1], left, dg_recv[4])
    arrived(whole(slot_part), dg_recv[0])
    send(whole(slot_part), whole(slot_part), right, dg_recv[5])
    send(whole(slot_part), whole(slot_part), left, dg_recv[6])
    combine()
    product(slot_l)
    product(slot_r)
    combine()
    combine()
    product(slot_part)
    combine()
    arrived(dg.at[slot_f, 0], dg_recv[3])
    arrived(dg.at[slot_f, 1], dg_recv[4])
    send(whole(slot_f), whole(slot_f), partner, dg_recv[7])

    arrived(hid_slot(slot_l), hid_recv[1])
    send(hid_slot(slot_l, 0), hid_slot(slot_l, 0), right, hid_recv[3])
    arrived(hid_slot(slot_r), hid_recv[2])
    send(hid_slot(slot_r, t), hid_slot(slot_r, t), left, hid_recv[4])
    arrived(hid_slot(slot_part), hid_recv[0])
    send(hid_slot(slot_part), hid_slot(slot_part), right, hid_recv[5])
    send(hid_slot(slot_part), hid_slot(slot_part), left, hid_recv[6])
    send(hid_slot(slot_l), hid_slot(slot_l), sibling, hid_sib_recv[1])
    send(hid_slot(slot_r), hid_slot(slot_r), sibling, hid_sib_recv[2])
    send(hid_slot(slot_part), hid_slot(slot_part), sibling, hid_sib_recv[3])

    product(slot_f)
    combine()
    arrived(whole(slot_lo), dg_recv[5])
    product(slot_lo)
    arrived(whole(slot_ro), dg_recv[6])
    product(slot_ro)
    combine()
    combine()
    arrived(whole(slot_fo), dg_recv[7])
    product(slot_fo)
    combine()

    for q in range(2):
        for step in range(1, 4):
            zz = lax.rem(z + step, 4)
            arrived(zr.at[q, zz], z_sems.at[q, zz])

    def over_z(q):
        return zr[q, 0].astype(F32) + zr[q, 1].astype(F32) + zr[q, 2].astype(F32) + zr[q, 3].astype(F32)

    dn_same, dn_other = new_recv(), new_recv()
    vs[0] = over_z(0).astype(BF16)
    vs[1] = over_z(1).astype(BF16)
    send(vs.at[b1], dn.at[1], perm_from(b1), dn_other)
    send(vs.at[b], dn.at[0], perm_from(b), dn_same, off_diagonal)

    @pl.when(diagonal)
    def _():
        dn[0] = vs[b]

    arrived(hid_slot(slot_f, 0), hid_recv[3])
    arrived(hid_slot(slot_f, t), hid_recv[4])
    send(hid_slot(slot_f), hid_slot(slot_f), partner, hid_recv[7])
    send(hid_slot(slot_f), hid_slot(slot_f), sibling, hid_sib_recv[4])

    @pl.when(off_diagonal)
    def _():
        arrived(dn.at[0], dn_same)

    arrived(dn.at[1], dn_other)
    scaled = (dn[0].astype(F32) + dn[1].astype(F32)) * gains[2]
    normed = mid[...].astype(F32) * inverse_mid_column
    inner = jnp.sum(scaled * normed, axis=1, keepdims=True)
    square[0:t, :] = jnp.broadcast_to(inner, (t, 128))
    fin[c] = jnp.transpose(square[...])[0:8, :]
    fin_recv = []
    for step in range(1, 8):
        fin_recv.append(new_recv())
        send(fin.at[c], fin.at[c], (r, lax.rem(c + step, 8)), fin_recv[-1])

    arrived(hid_slot(slot_lo), hid_recv[5])
    send(hid_slot(slot_lo), hid_slot(slot_lo), sibling, hid_sib_recv[5])
    arrived(hid_slot(slot_ro), hid_recv[6])
    send(hid_slot(slot_ro), hid_slot(slot_ro), sibling, hid_sib_recv[6])
    arrived(hid_slot(slot_fo), hid_recv[7])
    send(hid_slot(slot_fo), hid_slot(slot_fo), sibling, hid_sib_recv[7])

    for step in range(1, 8):
        arrived(fin.at[lax.rem(c + 8 - step, 8)], fin_recv[step - 1])
    total = fin[0]
    for i in range(1, 8):
        total = total + fin[i]
    square[0:8, :] = total
    inner_column = jnp.transpose(square[...])[0:t, 0:1]
    outv[...] = (
        outv[...].astype(F32) + inverse_mid_column * (scaled - normed * (inner_column / model))
    ).astype(BF16)
    final = fetch(outv, out_hbm)

    order = (slot_own, slot_l, slot_r, slot_part, slot_f, slot_lo, slot_ro, slot_fo)
    for slot, sem in zip(order, hid_sib_recv):
        arrived(hid_sib(slot), sem)
    own_hid.wait()
    dout_copy.wait()
    final.wait()
    for copy, when in sent:
        if when is None:
            copy.wait_send()
        else:
            pl.when(when)(copy.wait_send)


def local(
    block_out, stream_mid, gate_pre, up_pre, final_gain, mlp_gain, value_weight, returns, response_mask, w_gate, w_up, w_down
):
    t, width = block_out.shape
    units = gate_pre.shape[1]
    half, feat = units // 2, width // 2
    token_rows = jnp.pad(
        jnp.stack([returns, response_mask.astype(F32)]), ((0, 6), (0, 128 - t))
    )
    any_spec = pl.BlockSpec(memory_space=pl.ANY)
    vm = pltpu.VMEM
    out, hid, dout = pl.pallas_call(
        kernel,
        out_shape=(
            jax.ShapeDtypeStruct((t, width), BF16),
            jax.ShapeDtypeStruct((8, 2 * t, units), BF16),
            jax.ShapeDtypeStruct((16 * t, feat), BF16),
        ),
        in_specs=[any_spec] * 11,
        out_specs=(any_spec,) * 3,
        scratch_shapes=[
            vm((t, width), BF16),
            vm((t, width), BF16),
            vm((3, 1, width), F32),
            vm((8, 128), F32),
            vm((2, t, half), BF16),
            vm((2, t, half), BF16),
            vm((2, half, feat), BF16),
            vm((width, half), BF16),
            vm((width, half), BF16),
            vm((2 * t, half), F32),
            vm((2 * t, half), F32),
            vm((2 * t, half), BF16),
            vm((128, 128), F32),
            vm((8, 8, 128), F32),
            vm((128, 128), F32),
            vm((2, 8, t, width), BF16),
            vm((8, width), F32),
            vm((8, width), F32),
            vm((16 * t, width), BF16),
            vm((16 * t, half), BF16),
            vm((2 * t, half), BF16),
            vm((2 * t, half), BF16),
            vm((2 * t, half), BF16),
            vm((t, half), BF16),
            vm((t, half), BF16),
            vm((2 * t, half), BF16),
            vm((2 * t, half), BF16),
            vm((2 * t, half), BF16),
            vm((8, 2, 2 * t, half), BF16),
            vm((8, 2 * t, width), F32),
            vm((8, 2 * t, width), BF16),
            vm((8, t, width), BF16),
            vm((8, t, width), BF16),
            vm((2, 4, t, width), BF16),
            vm((2, t, width), BF16),
            vm((2, t, width), BF16),
            vm((8, 8, 128), F32),
            vm((t, width), BF16),
            pltpu.SemaphoreType.DMA((N_SEND,)),
            pltpu.SemaphoreType.DMA((N_RECV,)),
            pltpu.SemaphoreType.DMA((N_LOCAL,)),
            pltpu.SemaphoreType.DMA((2, 4)),
        ],
        compiler_params=pltpu.CompilerParams(
            collective_id=0, has_side_effects=True, vmem_limit_bytes=60 * 1024 * 1024
        ),
    )(
        block_out, stream_mid, gate_pre, up_pre,
        final_gain.reshape(1, width), mlp_gain.reshape(1, width), value_weight.reshape(1, width),
        token_rows, w_gate, w_up, w_down,
    )
    d_w_down = lax.dot_general(
        hid.reshape(16 * t, units), dout, (((0,), (0,)), ((), ())), preferred_element_type=F32
    )
    return out, d_w_down


def solution(mesh):
    placed = (
        P("row", "col"), P("row", "col"), P("row", "col"), P("row", "col"),
        P("col"), P("col"), P("col"), P("row"), P("row"),
        P("row", "col"), P("row", "col"), P("col", "row"),
    )
    return jax.shard_map(
        local, mesh=mesh, in_specs=placed, out_specs=(P("row", "col"), P("col", "row")), check_vma=False
    )
```

time: 505 us -> 161 us (0.32)
  waiting for transfers between devices: 266 us -> 0 us
  blocking collectives: 186 us -> 0 us
  Pallas kernels: 0 us -> 148 us
  between operations: 14.5 us -> 0.65 us
  matrix products: 22.7 us -> 8.89 us
  other arithmetic: 12 us -> 1.91 us
    reduce_scatter x2 -> x0, waiting for transfers between devices: 190 us -> none  [the longest x1 119 us: local(): lax.psum_scatter(contract(grad_rows, w_down, 1, 1), 'row', scatter_dimens...]
    pallas_call x0 -> x1, Pallas kernels: none -> 148 us  [local(): pl.pallas_call(kernel, out_shape=(jax.ShapeDtypeStruct((t, width), BF16),...]
    psum x4 -> x0, blocking collectives: 90.2 us -> none  [the longest x1 25.4 us: local(): lax.psum((jnp.sum(output_widened * output_widened, axis=1), jnp.sum(middl...]
    all_gather x2 -> x0, waiting for transfers between devices: 75.5 us -> none  [the longest x1 67.3 us: local(): piece = lax.all_gather(stacked, 'row', axis=1, tiled=True)]
    all_to_all x2 -> x0, blocking collectives: 59 us -> none  [the longest x1 38.1 us: local(): lax.all_to_all(normed_part, 'row', split_axis=0, concat_axis=1, tiled=True)]
    all_gather x1 -> x0, blocking collectives: 36.9 us -> none  [local(): full_rows = lax.all_gather(output_gradient, 'col', axis=1, tiled=True)]
    dot_general x4 -> x1, matrix products: 22.7 us -> 8.89 us  [local(): lax.dot_general(hid.reshape(16 * t, units), dout, (((0,), (0,)), ((), ())...]
  transfers between devices with their start and end apart: 4 -> 0, of which waited for: 4 -> 0; matrix products, arithmetic and copies ran while one was open for 4% -> 0% of each run, Pallas kernels for 0% -> 0%
where the time goes in v1:
time: 161 us
  Pallas kernels  148 us (92%)
  matrix products  8.89 us (6%)
  other arithmetic  1.91 us (1%)
    pallas_call x1, Pallas kernels, local(): pl.pallas_call(kernel, out_shape=(jax.ShapeDtypeStruct((t, width), BF16),...  148 us
    dot_general x1, matrix products, local(): lax.dot_general(hid.reshape(16 * t, units), dout, (((0,), (0,)), ((), ())...  8.89 us

profile of v1, /device:TPU:2, one launch (start us, length us, event | category | flops | bytes accessed | tf_op | source)
XLA Modules:
  0.0 160.6 jit_solution(9296153350648222323)
XLA Ops:
  0.6 0.7 convert_bitcast_fusion
  1.3 1.3 select_maximum_fusion.token_hbm
  2.5 148.5 %shard_map.131 = (bf16[48,1024]{1,0:T(8,128)(2,1)}, bf16[8,96,3584]{2,1,0:T(8,128)(2,1)}, bf16[768,512]{1,0:T(8,128)(2,1)}) custom-call(bf16[48,1024]{1,0:T(8,128)(2,1)} %block_hbm.1, bf16[48,1024]{1,0:T(8,128)(2,1)} %mid_hbm.1, bf16[48,3584]{1,0:T(8,128)(2,1)} %gate_hbm.1, bf16[48,3584]{1,0:T(8,128)(2,1)} %up_hbm.1, f32[1,1024]{1,0:T(1,128)} %bitcast.9, ...), custom_call_target="tpu_custom_call" | custom-call | tf_op jit(solution)/shard_map/pallas_call | solution.py:514
  151.0 0.0 copy-start
  151.0 8.9 %fusion = f32[3584,512]{1,0:T(8,128)} fusion(bf16[768,3584]{1,0:T(8,128)(2,1)} %bitcast.13, bf16[768,512]{1,0:T(8,128)(2,1)} %get-tuple-element.7), kind=kOutput, calls=%fused_computation.4 | convolution fusion | flops 2818572288 | bytes 13631488 | tf_op jit(solution)/shard_map/dot_general | solution.py:575
  159.9 0.0 copy-done
  159.9 0.6 copy.15
Async XLA Ops:
  151.0 8.9 %copy-start = (bf16[48,1024]{1,0:T(8,128)(2,1)S(1)}, bf16[48,1024]{1,0:T(8,128)(2,1)}, u32[]{:S(2)}) copy-start(bf16[48,1024]{1,0:T(8,128)(2,1)} %get-tuple-element.10) | copy-start | bytes 294916

commit v2 on v1

v2 whole, which is shorter than its diff:
```python
import functools
import math

import jax
import jax.numpy as jnp
from jax import lax
from jax.experimental import pallas as pl
from jax.experimental.pallas import tpu as pltpu
from jax.sharding import PartitionSpec as P

EPSILON = 1e-05
MESH = pl.DeviceIdType.MESH
F32 = jnp.float32
BF16 = jnp.bfloat16


def dot(left, right):
    return lax.dot_general(left, right, (((1,), (0,)), ((), ())), preferred_element_type=F32)


def hint(value, factor):
    return pl.multiple_of(value, factor)


class Sems:
    def __init__(self, ref):
        self.ref, self.used = ref, 0

    def __call__(self):
        self.used += 1
        return self.ref.at[self.used - 1]


N_SEND, N_RECV, N_LOCAL = 160, 160, 24


def kernel(
    block_hbm, mid_hbm, gate_hbm, up_hbm, final_gain, mlp_gain, value_weight, returns, mask, w_gate, w_up, w_down,
    out_hbm, hid, dout_hbm,
    blk, mid, gains, ret, msk, pack, gx, ux, wd, wg, wu, wdt, wgt, wut, fa, fb, hid_own,
    square, stat, share, tile, head, head_j, dout, part_sum,
    rf, nl, nr, ha, hb, ml, mr, my, dg, yf, yb, sb, zs, zr, vs, dn, fin, outv,
    send_sems, recv_sems, local_sems, z_sems, d_sems,
):
    t, width = blk.shape
    half = gx.shape[2]
    feat = width // 2
    tokens = 16 * t
    model = 8 * width
    first = (half // 2 + 255) // 256 * 256 if half >= 512 else half // 2
    pieces = (pl.ds(0, first), pl.ds(first, half - first))
    r, c = lax.axis_index("row"), lax.axis_index("col")
    k, j = lax.rem(r, 2), lax.div(r, 2)
    x, y = lax.div(j, 2), lax.rem(j, 2)
    z, b = lax.div(c, 2), lax.rem(c, 2)
    k1, y1, b1 = 1 - k, 1 - y, 1 - b
    xr, xl, xf = lax.rem(x + 1, 4), lax.rem(x + 3, 4), lax.rem(x + 2, 4)
    zp, zm, zf = lax.rem(z + 1, 4), lax.rem(z + 3, 4), lax.rem(z + 2, 4)
    sibling = (2 * j + k1, c)
    right, left = (4 * xr + 2 * y + k, c), (4 * xl + 2 * y + k, c)
    partner = (4 * x + 2 * y1 + k, c)
    z_plus, z_minus, z_partner = (r, 2 * zp + b), (r, 2 * zm + b), (r, 2 * z + b1)
    slot_own, slot_part = 2 * x + y, 2 * x + y1
    slot_l, slot_r, slot_f = 2 * xl + y, 2 * xr + y, 2 * xf + y
    slot_lo, slot_ro, slot_fo = 2 * xl + y1, 2 * xr + y1, 2 * xf + y1
    own_half = pl.ds(hint(k * half, 128), half)
    other_half = pl.ds(hint(k1 * half, 128), half)
    diagonal = j == c
    off_diagonal = j != c
    new_send, new_recv, new_local = Sems(send_sems), Sems(recv_sems), Sems(local_sems)
    sent = []

    def send(src, dst, to, recv, when=None):
        copy = pltpu.make_async_remote_copy(
            src_ref=src, dst_ref=dst, send_sem=new_send(), recv_sem=recv, device_id=to, device_id_type=MESH
        )
        if when is None:
            copy.start()
        else:
            pl.when(when)(copy.start)
        sent.append((copy, when))

    def send_same(ref, to, recv):
        send(ref, ref, to, recv)

    def arrived(dst, recv):
        pltpu.make_async_copy(dst, dst, recv).wait()

    def fetch(src, dst):
        copy = pltpu.make_async_copy(src, dst, new_local())
        copy.start()
        return copy

    barrier = pltpu.get_barrier_semaphore()

    def greet(device):
        pl.semaphore_signal(barrier, inc=1, device_id=device, device_id_type=MESH)

    def perm_to(which):
        return (2 * c + k, 2 * x + which)

    def perm_from(which):
        return (2 * (2 * z + which) + k, j)

    greet(perm_to(y1))
    greet(perm_from(b1))

    @pl.when(off_diagonal)
    def _():
        greet(perm_to(y))
        greet(perm_from(b))

    for step in (4, 5, 3, 6, 2, 7, 1):
        greet((r, lax.rem(c + step, 8)))
    for step in (8, 9, 7, 10, 6, 11, 5, 12, 4, 13, 3, 14, 2, 15, 1):
        greet((lax.rem(r + step, 16), c))

    small = [
        fetch(block_hbm, blk),
        fetch(mid_hbm, mid),
        fetch(final_gain, gains.at[0]),
        fetch(value_weight, gains.at[1]),
        fetch(mlp_gain, gains.at[2]),
        fetch(returns, ret),
        fetch(mask, msk),
    ]
    halves = [fetch(gate_hbm.at[:, own_half], gx.at[k]), fetch(up_hbm.at[:, own_half], ux.at[k])]
    own_rows = pl.ds(hint(k * feat, 16), feat)
    weights_down = fetch(w_down.at[own_half, :], wd.at[k])
    weights_in = [fetch(w_gate.at[:, own_half], wg.at[own_rows]), fetch(w_up.at[:, own_half], wu.at[own_rows])]
    for copy in small:
        copy.wait()

    lane = lax.broadcasted_iota(jnp.int32, (t, 128), 1)
    head[...] = gains[0] * gains[1]
    block_wide = blk[...].astype(F32)
    mid_wide = mid[...].astype(F32)
    square[...] = jnp.zeros_like(square)
    pack[...] = jnp.zeros_like(pack)
    sum_out = jnp.sum(block_wide * block_wide, axis=1, keepdims=True)
    sum_head = jnp.sum(block_wide * head[...], axis=1, keepdims=True)
    sum_mid = jnp.sum(mid_wide * mid_wide, axis=1, keepdims=True)
    square[0:t, :] = jnp.where(
        lane == 0, sum_out, jnp.where(lane == 1, sum_head, jnp.where(lane == 2, sum_mid, 0.0))
    )
    stat[c] = jnp.transpose(square[...])[0:8, :]

    @pl.when(off_diagonal)
    def _():
        pl.semaphore_wait(barrier, 26)

    @pl.when(diagonal)
    def _():
        pl.semaphore_wait(barrier, 24)

    stat_recv = {}
    for step in (4, 5, 3, 6, 2, 7, 1):
        stat_recv[step] = new_recv()
        send_same(stat.at[c], (r, lax.rem(c + step, 8)), stat_recv[step])
    perm_recv, perm_head = new_recv(), new_recv()
    send(block_hbm, tile.at[k, j], perm_to(y), perm_recv, off_diagonal)
    send(head, head_j, perm_to(y), perm_head, off_diagonal)

    @pl.when(diagonal)
    def _():
        tile[k, j] = blk[...]
        head_j[...] = head[...]

    gate_recv, up_recv, wd_recv, wg_recv, wu_recv = (new_recv() for _ in range(5))
    send(gate_hbm.at[:, other_half], gx.at[k], sibling, gate_recv)
    send(up_hbm.at[:, other_half], ux.at[k], sibling, up_recv)
    send(w_down.at[other_half, :], wd.at[k], sibling, wd_recv)

    for copy in halves:
        copy.wait()
    arrived(gx.at[k1], gate_recv)
    arrived(ux.at[k1], up_recv)
    for q in range(2):

        @pl.loop(0, t // 16)
        def _(i):
            rows = pl.ds(hint(i * 16, 16), 16)
            out_rows = pl.ds(hint(q * t + i * 16, 16), 16)
            gate, up = gx[q, rows, :].astype(F32), ux[q, rows, :].astype(F32)
            sig = jax.nn.sigmoid(gate)
            silu = gate * sig
            fa[out_rows, :] = up * sig * (1.0 + gate * (1.0 - sig))
            fb[out_rows, :] = silu
            hid_own[out_rows, :] = (silu * up).astype(BF16)

    def hid_slot(slot, rows=None):
        return hid.at[slot, :, own_half] if rows is None else hid.at[slot, pl.ds(rows, t), own_half]

    hid_recv = [new_recv() for _ in range(8)]
    hid_sib = []

    def hid_to_sibling(slot):
        hid_sib.append((slot, new_recv()))
        send_same(hid_slot(slot), sibling, hid_sib[-1][1])

    own_hid = fetch(hid_own, hid_slot(slot_own))
    send(hid_own, hid_slot(slot_own), partner, hid_recv[0])
    send(hid_own, hid_slot(slot_own), right, hid_recv[1])
    send(hid_own, hid_slot(slot_own), left, hid_recv[2])

    for step in (1, 7, 2, 6, 3, 5, 4):
        arrived(stat.at[lax.rem(c + 8 - step, 8)], stat_recv[step])
    total = stat[0]
    for i in range(1, 8):
        total = total + stat[i]
    total = total[:, 0:t]
    inverse_out = lax.rsqrt(total[0:1] / model + EPSILON)
    value = inverse_out * total[1:2]
    live = msk[...].astype(F32)
    slope = inverse_out * (live * (value - ret[...]))
    pack[0:1, 0:t] = slope
    pack[1:2, 0:t] = -slope * inverse_out * value / model
    pack[2:3, 0:t] = live
    pack[3:4, 0:t] = lax.rsqrt(total[2:3] / model + EPSILON)
    own_share = pl.ds(hint(8 * r, 8), 8)
    share[own_share, :] = pack[...]
    share_recv = {}
    for step in (8, 9, 7, 10, 6, 11, 5, 12, 4, 13, 3, 14, 2, 15, 1):
        share_recv[step] = new_recv()
        send_same(share.at[own_share], (lax.rem(r + step, 16), c), share_recv[step])

    sib_tile = []

    def tile_to_sibling(slot):
        sib_tile.append((slot, new_recv()))
        send_same(tile.at[k, slot], sibling, sib_tile[-1][1])

    t_part, t_own_m, t_own_p, t_oth_m, t_oth_p, t_far_own, t_far_oth = (new_recv() for _ in range(7))

    @pl.when(off_diagonal)
    def _():
        arrived(tile.at[k, c], perm_recv)
        arrived(head_j, perm_head)

    send_same(tile.at[k, c], z_partner, t_part)
    send_same(tile.at[k, c], z_plus, t_own_m)
    send_same(tile.at[k, c], z_minus, t_own_p)
    tile_to_sibling(c)

    weights_down.wait()
    arrived(wd.at[k1], wd_recv)
    u_tile = 256 if half % 256 == 0 else 128
    for q in range(2):

        @pl.loop(0, half // u_tile)
        def _(n):
            units = pl.ds(hint(n * u_tile, 128), u_tile)
            wdt[q * feat : (q + 1) * feat, units] = jnp.transpose(wd[q, units, :])

    arrived(tile.at[k, 2 * zm + b], t_own_m)
    send_same(tile.at[k, 2 * zm + b], z_plus, t_far_own)
    tile_to_sibling(2 * zm + b)
    arrived(tile.at[k, 2 * z + b1], t_part)
    send_same(tile.at[k, 2 * z + b1], z_plus, t_oth_m)
    send_same(tile.at[k, 2 * z + b1], z_minus, t_oth_p)
    tile_to_sibling(2 * z + b1)
    arrived(tile.at[k, 2 * zp + b], t_own_p)
    tile_to_sibling(2 * zp + b)

    arrived(hid_slot(slot_l), hid_recv[1])
    send_same(hid_slot(slot_l, 0), right, hid_recv[3])
    arrived(hid_slot(slot_r), hid_recv[2])
    send_same(hid_slot(slot_r, t), left, hid_recv[4])
    arrived(hid_slot(slot_part), hid_recv[0])
    send_same(hid_slot(slot_part), right, hid_recv[5])
    send_same(hid_slot(slot_part), left, hid_recv[6])

    arrived(tile.at[k, 2 * zp + b1], t_oth_p)
    send_same(tile.at[k, 2 * zp + b1], z_minus, t_far_oth)
    tile_to_sibling(2 * zp + b1)
    arrived(tile.at[k, 2 * zm + b1], t_oth_m)
    tile_to_sibling(2 * zm + b1)
    arrived(tile.at[k, 2 * zf + b], t_far_own)
    tile_to_sibling(2 * zf + b)

    for step in (1, 15, 2, 14, 3, 13, 4, 12, 5, 11, 6, 10, 7, 9, 8):
        from_row = lax.rem(r + 16 - step, 16)
        arrived(share.at[pl.ds(hint(8 * from_row, 8), 8)], share_recv[step])
    shares = share[...]
    which = lax.rem(lax.broadcasted_iota(jnp.int32, (128, 128), 0), 8)
    count = jnp.sum(jnp.sum(jnp.where(which == 2, shares, 0.0), axis=0, keepdims=True), axis=1, keepdims=True)
    factor = tokens * math.sqrt(model) / count
    columns = jnp.transpose(shares) * factor
    square[0:8, :] = pack[...]
    own_columns = jnp.transpose(square[...])

    arrived(tile.at[k, 2 * zf + b1], t_far_oth)
    tile_to_sibling(2 * zf + b1)
    send(w_gate.at[:, other_half], wg.at[own_rows], sibling, wg_recv)
    send(w_up.at[:, other_half], wu.at[own_rows], sibling, wu_recv)
    for slot, sem in sib_tile:
        arrived(tile.at[k1, slot], sem)

    head_row = head_j[...]
    for s in range(8):
        for q in range(2):
            at = 8 * (2 * s + q)
            dout[(2 * s + q) * t : (2 * s + q + 1) * t, :] = (
                columns[0:t, at : at + 1] * head_row + columns[0:t, at + 1 : at + 2] * tile[q, s].astype(F32)
            ).astype(BF16)
    dout_copy = fetch(dout.at[:, pl.ds(hint(k * feat, 128), feat)], dout_hbm)

    def chunk(slot, piece, start=0, size=2 * t):
        return part_sum.at[pl.ds(hint(slot * 2 * t + start, 16), size), piece]

    def hidden(slot, piece):
        rows = pl.ds(hint(slot * 2 * t, 16), 2 * t)
        part_sum[rows, piece] = dot(dout[rows, :], wdt[:, piece]).astype(BF16)

    def add_into(slot, piece, others, start=0, size=2 * t):
        @pl.loop(0, size // 16)
        def _(i):
            rows = pl.ds(hint(slot * 2 * t + start + i * 16, 16), 16)
            their = pl.ds(hint(i * 16, 16), 16)
            value = part_sum[rows, piece].astype(F32)
            for other in others:
                value = value + other[their, piece].astype(F32)
            part_sum[rows, piece] = value.astype(BF16)

    both = (0, 1)
    rf_s, nl_s, nr_s, ha_s, hb_s, ml_s, mr_s, my_s = ([new_recv(), new_recv()] for _ in range(8))
    for h in both:
        hidden(slot_fo, pieces[h])
        send(chunk(slot_fo, pieces[h]), rf.at[:, pieces[h]], partner, rf_s[h])
        hidden(slot_ro, pieces[h])
        send(chunk(slot_ro, pieces[h]), nl.at[:, pieces[h]], right, nl_s[h])
        hidden(slot_lo, pieces[h])
        send(chunk(slot_lo, pieces[h]), nr.at[:, pieces[h]], left, nr_s[h])
    for h in both:
        hidden(slot_f, pieces[h])
        arrived(rf.at[:, pieces[h]], rf_s[h])
        add_into(slot_f, pieces[h], (rf,))
        send(chunk(slot_f, pieces[h], 0, t), ha.at[:, pieces[h]], right, ha_s[h])
        send(chunk(slot_f, pieces[h], t, t), hb.at[:, pieces[h]], left, hb_s[h])
    for h in both:
        hidden(slot_part, pieces[h])
    for h in both:
        hidden(slot_r, pieces[h])
        hidden(slot_l, pieces[h])
        arrived(nl.at[:, pieces[h]], nl_s[h])
        arrived(nr.at[:, pieces[h]], nr_s[h])
        add_into(slot_part, pieces[h], (nl, nr))
        send(chunk(slot_part, pieces[h]), my.at[:, pieces[h]], partner, my_s[h])
    for h in both:
        arrived(ha.at[:, pieces[h]], ha_s[h])
        add_into(slot_r, pieces[h], (ha,), 0, t)
        send(chunk(slot_r, pieces[h]), ml.at[:, pieces[h]], right, ml_s[h])
        arrived(hb.at[:, pieces[h]], hb_s[h])
        add_into(slot_l, pieces[h], (hb,), t, t)
        send(chunk(slot_l, pieces[h]), mr.at[:, pieces[h]], left, mr_s[h])
    for h in both:
        hidden(slot_own, pieces[h])

    arrived(hid_slot(slot_f, 0), hid_recv[3])
    arrived(hid_slot(slot_f, t), hid_recv[4])
    send_same(hid_slot(slot_f), partner, hid_recv[7])
    own_hid.wait()
    for slot in (slot_own, slot_l, slot_r, slot_part, slot_f):
        hid_to_sibling(slot)
    for copy in weights_in:
        copy.wait()
    other_rows = pl.ds(hint(k1 * feat, 16), feat)
    f_tile = 256 if width % 256 == 0 else 128
    for source, target, sem in ((wg, wgt, wg_recv), (wu, wut, wu_recv)):
        arrived(source.at[other_rows], sem)

        @pl.loop(0, width // f_tile)
        def _(n):
            features = pl.ds(hint(n * f_tile, 128), f_tile)
            target[:, features] = jnp.transpose(source[features, :])

    inverse_mid_column = own_columns[0:t, 3:4]
    outv[...] = (
        (own_columns[0:t, 0:1] * factor) * head[...] + (own_columns[0:t, 1:2] * factor) * blk[...].astype(F32)
    ).astype(BF16)

    dg_recv = [[new_recv(), new_recv()] for _ in range(8)]
    sb_recv = [new_recv() for _ in range(8)]
    pending, last = [], []

    def whole(slot, piece):
        return dg.at[slot, :, :, piece]

    def one(slot, which, piece):
        return dg.at[slot, which, :, piece]

    for h in both:
        piece = pieces[h]
        arrived(my.at[:, piece], my_s[h])
        arrived(ml.at[:, piece], ml_s[h])
        arrived(mr.at[:, piece], mr_s[h])

        @pl.loop(0, 2 * t // 16)
        def _(i):
            rows = pl.ds(hint(i * 16, 16), 16)
            d_hidden = (
                part_sum[pl.ds(hint(slot_own * 2 * t + i * 16, 16), 16), piece].astype(F32)
                + ml[rows, piece].astype(F32)
                + mr[rows, piece].astype(F32)
                + my[rows, piece].astype(F32)
            )
            dg[slot_own, 0, rows, piece] = (d_hidden * fa[rows, piece]).astype(BF16)
            dg[slot_own, 1, rows, piece] = (d_hidden * fb[rows, piece]).astype(BF16)

        send_same(whole(slot_own, piece), right, dg_recv[1][h])
        send_same(whole(slot_own, piece), left, dg_recv[2][h])
        send_same(whole(slot_own, piece), partner, dg_recv[0][h])

    def product(slot, h):
        piece = pieces[h]
        value = dot(dg[slot, 0, :, piece], wgt[piece, :]) + dot(dg[slot, 1, :, piece], wut[piece, :])
        if h == 0:
            yf[slot] = value
            return
        value = value + yf[slot]
        yf[slot] = value
        yb[slot] = value.astype(BF16)
        sem = sb_recv[len(last) + len(pending)]
        send(yb.at[slot, pl.ds(hint(k1 * t, 16), t)], sb.at[slot], sibling, sem)
        pending.append((slot, sem))

    def combine():
        slot, sem = pending.pop(0)
        arrived(sb.at[slot], sem)
        zz, bb = lax.div(slot, 2), lax.rem(slot, 2)
        summed = (yf[slot, pl.ds(hint(k * t, 16), t), :] + sb[slot].astype(F32)).astype(BF16)
        zs[slot] = summed
        send(zs.at[slot], zr.at[bb, z], (r, 2 * zz + b), z_sems.at[bb, z], zz != z)

        @pl.when(zz == z)
        def _():
            zr[bb, z] = summed

        last.append(slot)

    def over_z(q):
        for step in range(1, 4):
            zz = lax.rem(z + step, 4)
            arrived(zr.at[q, zz], z_sems.at[q, zz])
        vs[q] = (
            zr[q, 0].astype(F32) + zr[q, 1].astype(F32) + zr[q, 2].astype(F32) + zr[q, 3].astype(F32)
        ).astype(BF16)

    product(slot_own, 0)
    product(slot_own, 1)
    for h in both:
        arrived(whole(slot_l, pieces[h]), dg_recv[1][h])
        send_same(one(slot_l, 0, pieces[h]), right, dg_recv[3][h])
        arrived(whole(slot_r, pieces[h]), dg_recv[2][h])
        send_same(one(slot_r, 1, pieces[h]), left, dg_recv[4][h])
        if h == 0:
            combine()
            product(slot_l, 0)
            product(slot_r, 0)
    for h in both:
        arrived(whole(slot_part, pieces[h]), dg_recv[0][h])
        send_same(whole(slot_part, pieces[h]), right, dg_recv[5][h])
        send_same(whole(slot_part, pieces[h]), left, dg_recv[6][h])
    product(slot_l, 1)
    product(slot_r, 1)
    for h in both:
        arrived(one(slot_f, 0, pieces[h]), dg_recv[3][h])
        arrived(one(slot_f, 1, pieces[h]), dg_recv[4][h])
        send_same(whole(slot_f, pieces[h]), partner, dg_recv[7][h])
        if h == 0:
            combine()
            product(slot_part, 0)
            product(slot_part, 1)
            combine()
        product(slot_f, h)
    combine()
    combine()

    same = lax.rem(y + b, 2)
    over_z(y)
    send(vs.at[y], dn.at[same], perm_from(y), d_sems.at[same], off_diagonal)

    @pl.when(diagonal)
    def _():
        dn[same] = vs[y]

    arrived(hid_slot(slot_lo), hid_recv[5])
    hid_to_sibling(slot_lo)
    arrived(hid_slot(slot_ro), hid_recv[6])
    hid_to_sibling(slot_ro)
    arrived(hid_slot(slot_fo), hid_recv[7])
    hid_to_sibling(slot_fo)

    for h in both:
        arrived(whole(slot_fo, pieces[h]), dg_recv[7][h])
        product(slot_fo, h)
        arrived(whole(slot_lo, pieces[h]), dg_recv[5][h])
        product(slot_lo, h)
        arrived(whole(slot_ro, pieces[h]), dg_recv[6][h])
        product(slot_ro, h)
    combine()
    combine()
    combine()
    over_z(y1)
    send(vs.at[y1], dn.at[1 - same], perm_from(y1), d_sems.at[1 - same])

    for slot, sem in hid_sib:
        arrived(hid.at[slot, :, other_half], sem)

    @pl.when(off_diagonal)
    def _():
        arrived(dn.at[0], d_sems.at[0])

    arrived(dn.at[1], d_sems.at[1])
    scaled = (dn[0].astype(F32) + dn[1].astype(F32)) * gains[2]
    normed = mid[...].astype(F32) * inverse_mid_column
    inner = jnp.sum(scaled * normed, axis=1, keepdims=True)
    square[0:t, :] = jnp.broadcast_to(inner, (t, 128))
    fin[c] = jnp.transpose(square[...])[0:8, :]
    fin_recv = {}
    for step in (4, 5, 3, 6, 2, 7, 1):
        fin_recv[step] = new_recv()
        send_same(fin.at[c], (r, lax.rem(c + step, 8)), fin_recv[step])
    for step in (1, 7, 2, 6, 3, 5, 4):
        arrived(fin.at[lax.rem(c + 8 - step, 8)], fin_recv[step])
    total = fin[0]
    for i in range(1, 8):
        total = total + fin[i]
    square[0:8, :] = total
    inner_column = jnp.transpose(square[...])[0:t, 0:1]
    outv[...] = (
        outv[...].astype(F32) + inverse_mid_column * (scaled - normed * (inner_column / model))
    ).astype(BF16)
    final = fetch(outv, out_hbm)
    dout_copy.wait()
    final.wait()
    for copy, when in sent:
        if when is None:
            copy.wait_send()
        else:
            pl.when(when)(copy.wait_send)


def local(
    block_out, stream_mid, gate_pre, up_pre, final_gain, mlp_gain, value_weight, returns, response_mask, w_gate, w_up, w_down
):
    t, width = block_out.shape
    units = gate_pre.shape[1]
    half, feat = units // 2, width // 2
    any_spec = pl.BlockSpec(memory_space=pl.ANY)
    vm = pltpu.VMEM
    out, hid, dout = pl.pallas_call(
        kernel,
        out_shape=(
            jax.ShapeDtypeStruct((t, width), BF16),
            jax.ShapeDtypeStruct((8, 2 * t, units), BF16),
            jax.ShapeDtypeStruct((16 * t, feat), BF16),
        ),
        in_specs=[any_spec] * 12,
        out_specs=(any_spec,) * 3,
        scratch_shapes=[
            vm((t, width), BF16),
            vm((t, width), BF16),
            vm((3, 1, width), F32),
            vm((1, t), F32),
            vm((1, t), jnp.int32),
            vm((8, 128), F32),
            vm((2, t, half), BF16),
            vm((2, t, half), BF16),
            vm((2, half, feat), BF16),
            vm((width, half), BF16),
            vm((width, half), BF16),
            vm((width, half), BF16),
            vm((half, width), BF16),
            vm((half, width), BF16),
            vm((2 * t, half), F32),
            vm((2 * t, half), F32),
            vm((2 * t, half), BF16),
            vm((128, 128), F32),
            vm((8, 8, 128), F32),
            vm((128, 128), F32),
            vm((2, 8, t, width), BF16),
            vm((1, width), F32),
            vm((1, width), F32),
            vm((16 * t, width), BF16),
            vm((16 * t, half), BF16),
            vm((2 * t, half), BF16),
            vm((2 * t, half), BF16),
            vm((2 * t, half), BF16),
            vm((t, half), BF16),
            vm((t, half), BF16),
            vm((2 * t, half), BF16),
            vm((2 * t, half), BF16),
            vm((2 * t, half), BF16),
            vm((8, 2, 2 * t, half), BF16),
            vm((8, 2 * t, width), F32),
            vm((8, 2 * t, width), BF16),
            vm((8, t, width), BF16),
            vm((8, t, width), BF16),
            vm((2, 4, t, width), BF16),
            vm((2, t, width), BF16),
            vm((2, t, width), BF16),
            vm((8, 8, 128), F32),
            vm((t, width), BF16),
            pltpu.SemaphoreType.DMA((N_SEND,)),
            pltpu.SemaphoreType.DMA((N_RECV,)),
            pltpu.SemaphoreType.DMA((N_LOCAL,)),
            pltpu.SemaphoreType.DMA((2, 4)),
            pltpu.SemaphoreType.DMA((2,)),
        ],
        compiler_params=pltpu.CompilerParams(
            collective_id=0, has_side_effects=True, vmem_limit_bytes=60 * 1024 * 1024
        ),
    )(
        block_out, stream_mid, gate_pre, up_pre,
        final_gain.reshape(1, width), mlp_gain.reshape(1, width), value_weight.reshape(1, width),
        returns.reshape(1, t), response_mask.reshape(1, t), w_gate, w_up, w_down,
    )
    d_w_down = lax.dot_general(
        hid.reshape(16 * t, units), dout, (((0,), (0,)), ((), ())), preferred_element_type=F32
    )
    return out, d_w_down


def solution(mesh):
    placed = (
        P("row", "col"), P("row", "col"), P("row", "col"), P("row", "col"),
        P("col"), P("col"), P("col"), P("row"), P("row"),
        P("row", "col"), P("row", "col"), P("col", "row"),
    )
    return jax.shard_map(
        local, mesh=mesh, in_specs=placed, out_specs=(P("row", "col"), P("col", "row")), check_vma=False
    )
```

time: 161 us -> 136 us (0.84); the launches traced: 161 us -> 134 us
  Pallas kernels: 148 us -> 124 us
  other arithmetic: 1.91 us -> 0 us
    pallas_call x1, Pallas kernels: 148 us -> 124 us  [local(): pl.pallas_call(kernel, out_shape=(jax.ShapeDtypeStruct((t, width), BF16),...]
    another operation x2 -> x0, other arithmetic: 1.91 us -> none  [local(): jnp.stack([returns, response_mask.astype(F32)])]
where the time goes in v2:
time: 136 us; the launch traced here: 134 us
  Pallas kernels  124 us (91%)
  matrix products  8.89 us (7%)
    pallas_call x1, Pallas kernels, local(): pl.pallas_call(kernel, out_shape=(jax.ShapeDtypeStruct((t, width), BF16),...  124 us
    dot_general x1, matrix products, local(): lax.dot_general(hid.reshape(16 * t, units), dout, (((0,), (0,)), ((), ())...  8.89 us

profile of v2, /device:TPU:2, one launch (start us, length us, event | category | flops | bytes accessed | tf_op | source)
XLA Modules:
  0.0 133.9 jit_solution(4349560366098205449)
XLA Ops:
  0.6 123.7 %shard_map.131 = (bf16[48,1024]{1,0:T(8,128)(2,1)}, bf16[8,96,3584]{2,1,0:T(8,128)(2,1)}, bf16[768,512]{1,0:T(8,128)(2,1)}) custom-call(bf16[48,1024]{1,0:T(8,128)(2,1)} %block_hbm.1, bf16[48,1024]{1,0:T(8,128)(2,1)} %mid_hbm.1, bf16[48,3584]{1,0:T(8,128)(2,1)} %gate_hbm.1, bf16[48,3584]{1,0:T(8,128)(2,1)} %up_hbm.1, f32[1,1024]{1,0:T(1,128)} %bitcast.8, ...), custom_call_target="tpu_custom_call" | custom-call | tf_op jit(solution)/shard_map/pallas_call | solution.py:552
  124.4 0.0 copy-start
  124.4 8.9 %fusion = f32[3584,512]{1,0:T(8,128)} fusion(bf16[768,3584]{1,0:T(8,128)(2,1)} %bitcast.13, bf16[768,512]{1,0:T(8,128)(2,1)} %get-tuple-element.7), kind=kOutput, calls=%fused_computation | convolution fusion | flops 2818572288 | bytes 13631488 | tf_op jit(solution)/shard_map/dot_general | solution.py:619
  133.3 0.0 copy-done
  133.3 0.6 copy.15
Async XLA Ops:
  124.4 8.9 %copy-start = (bf16[48,1024]{1,0:T(8,128)(2,1)S(1)}, bf16[48,1024]{1,0:T(8,128)(2,1)}, u32[]{:S(2)}) copy-start(bf16[48,1024]{1,0:T(8,128)(2,1)} %get-tuple-element.10) | copy-start | bytes 294916

commit v3 on v2

--- a/solution.py
+++ b/solution.py
@@ -36,7 +36,7 @@
 
 def kernel(
     block_hbm, mid_hbm, gate_hbm, up_hbm, final_gain, mlp_gain, value_weight, returns, mask, w_gate, w_up, w_down,
-    out_hbm, hid, dout_hbm,
+    out_hbm, hid, dw_hbm,
     blk, mid, gains, ret, msk, pack, gx, ux, wd, wg, wu, wdt, wgt, wut, fa, fb, hid_own,
     square, stat, share, tile, head, head_j, dout, part_sum,
     rf, nl, nr, ha, hb, ml, mr, my, dg, yf, yb, sb, zs, zr, vs, dn, fin, outv,
@@ -99,16 +99,31 @@
     def perm_to(which):
         return (2 * c + k, 2 * x + which)
 
-    def perm_from(which):
-        return (2 * (2 * z + which) + k, j)
-
-    greet(perm_to(y1))
-    greet(perm_from(b1))
+    def perm_from():
+        return (2 * c + k, j)
+
+    sum_x = lax.rem(z + 4 - x, 4)
+    own_sum = jnp.logical_and(diagonal, x == 0)
+    not_own_sum = jnp.logical_not(own_sum)
+
+    def sum_to(which):
+        return (2 * (2 * sum_x + which) + k, j)
+
+    def sum_from(which):
+        return (2 * c + k, 2 * lax.rem(x + z, 4) + which)
+
+    greet(sum_to(b1))
+    greet(sum_from(y1))
+
+    @pl.when(not_own_sum)
+    def _():
+        greet(sum_to(b))
+        greet(sum_from(y))
 
     @pl.when(off_diagonal)
     def _():
         greet(perm_to(y))
-        greet(perm_from(b))
+        greet(perm_from())
 
     for step in (4, 5, 3, 6, 2, 7, 1):
         greet((r, lax.rem(c + step, 8)))
@@ -147,9 +162,13 @@
 
     @pl.when(off_diagonal)
     def _():
+        pl.semaphore_wait(barrier, 28)
+
+    @pl.when(jnp.logical_and(diagonal, x != 0))
+    def _():
         pl.semaphore_wait(barrier, 26)
 
-    @pl.when(diagonal)
+    @pl.when(own_sum)
     def _():
         pl.semaphore_wait(barrier, 24)
 
@@ -189,9 +208,10 @@
             hid_own[out_rows, :] = (silu * up).astype(BF16)
 
     def hid_slot(slot, rows=None):
-        return hid.at[slot, :, own_half] if rows is None else hid.at[slot, pl.ds(rows, t), own_half]
-
-    hid_recv = [new_recv() for _ in range(8)]
+        size = 2 * t if rows is None else t
+        return hid.at[pl.ds(hint(slot * 2 * t + (rows or 0), 16), size), own_half]
+
+    hid_recv = [new_recv() for _ in range(10)]
     hid_sib = []
 
     def hid_to_sibling(slot):
@@ -199,7 +219,6 @@
         send_same(hid_slot(slot), sibling, hid_sib[-1][1])
 
     own_hid = fetch(hid_own, hid_slot(slot_own))
-    send(hid_own, hid_slot(slot_own), partner, hid_recv[0])
     send(hid_own, hid_slot(slot_own), right, hid_recv[1])
     send(hid_own, hid_slot(slot_own), left, hid_recv[2])
 
@@ -241,6 +260,7 @@
     send_same(tile.at[k, c], z_plus, t_own_m)
     send_same(tile.at[k, c], z_minus, t_own_p)
     tile_to_sibling(c)
+    send(hid_own, hid_slot(slot_own), partner, hid_recv[0])
 
     weights_down.wait()
     arrived(wd.at[k1], wd_recv)
@@ -262,19 +282,17 @@
     arrived(tile.at[k, 2 * zp + b], t_own_p)
     tile_to_sibling(2 * zp + b)
 
-    arrived(hid_slot(slot_l), hid_recv[1])
-    send_same(hid_slot(slot_l, 0), right, hid_recv[3])
-    arrived(hid_slot(slot_r), hid_recv[2])
-    send_same(hid_slot(slot_r, t), left, hid_recv[4])
-    arrived(hid_slot(slot_part), hid_recv[0])
-    send_same(hid_slot(slot_part), right, hid_recv[5])
-    send_same(hid_slot(slot_part), left, hid_recv[6])
-
     arrived(tile.at[k, 2 * zp + b1], t_oth_p)
     send_same(tile.at[k, 2 * zp + b1], z_minus, t_far_oth)
     tile_to_sibling(2 * zp + b1)
     arrived(tile.at[k, 2 * zm + b1], t_oth_m)
     tile_to_sibling(2 * zm + b1)
+    arrived(hid_slot(slot_l), hid_recv[1])
+    send_same(hid_slot(slot_l, 0), right, hid_recv[3])
+    send_same(hid_slot(slot_l, t), partner, hid_recv[8])
+    arrived(hid_slot(slot_r), hid_recv[2])
+    send_same(hid_slot(slot_r, t), left, hid_recv[4])
+    send_same(hid_slot(slot_r, t), partner, hid_recv[9])
     arrived(tile.at[k, 2 * zf + b], t_far_own)
     tile_to_sibling(2 * zf + b)
 
@@ -293,6 +311,9 @@
     tile_to_sibling(2 * zf + b1)
     send(w_gate.at[:, other_half], wg.at[own_rows], sibling, wg_recv)
     send(w_up.at[:, other_half], wu.at[own_rows], sibling, wu_recv)
+    arrived(hid_slot(slot_part), hid_recv[0])
+    send_same(hid_slot(slot_part, 0), right, hid_recv[5])
+    send_same(hid_slot(slot_part, 0), left, hid_recv[6])
     for slot, sem in sib_tile:
         arrived(tile.at[k1, slot], sem)
 
@@ -303,7 +324,6 @@
             dout[(2 * s + q) * t : (2 * s + q + 1) * t, :] = (
                 columns[0:t, at : at + 1] * head_row + columns[0:t, at + 1 : at + 2] * tile[q, s].astype(F32)
             ).astype(BF16)
-    dout_copy = fetch(dout.at[:, pl.ds(hint(k * feat, 128), feat)], dout_hbm)
 
     def chunk(slot, piece, start=0, size=2 * t):
         return part_sum.at[pl.ds(hint(slot * 2 * t + start, 16), size), piece]
@@ -360,7 +380,11 @@
     arrived(hid_slot(slot_f, t), hid_recv[4])
     send_same(hid_slot(slot_f), partner, hid_recv[7])
     own_hid.wait()
-    for slot in (slot_own, slot_l, slot_r, slot_part, slot_f):
+    arrived(hid_slot(slot_lo, 0), hid_recv[5])
+    arrived(hid_slot(slot_ro, 0), hid_recv[6])
+    arrived(hid_slot(slot_lo, t), hid_recv[8])
+    arrived(hid_slot(slot_ro, t), hid_recv[9])
+    for slot in (slot_own, slot_l, slot_r, slot_part, slot_f, slot_lo, slot_ro):
         hid_to_sibling(slot)
     for copy in weights_in:
         copy.wait()
@@ -379,12 +403,20 @@
         (own_columns[0:t, 0:1] * factor) * head[...] + (own_columns[0:t, 1:2] * factor) * blk[...].astype(F32)
     ).astype(BF16)
 
-    dg_recv = [[new_recv(), new_recv()] for _ in range(8)]
+    dg_recv = [[new_recv(), new_recv()] for _ in range(10)]
     sb_recv = [new_recv() for _ in range(8)]
     pending, last = [], []
 
     def whole(slot, piece):
         return dg.at[slot, :, :, piece]
+
+    cut = 2 * t - 16
+
+    def most(slot, piece):
+        return dg.at[slot, :, 0:cut, piece]
+
+    def rest(slot, piece):
+        return dg.at[slot, :, cut:, piece]
 
     def one(slot, which, piece):
         return dg.at[slot, which, :, piece]
@@ -427,7 +459,7 @@
     def combine():
         slot, sem = pending.pop(0)
         arrived(sb.at[slot], sem)
-        zz, bb = lax.div(slot, 2), lax.rem(slot, 2)
+        zz, bb = lax.rem(lax.div(slot, 2) + x, 4), lax.rem(slot, 2)
         summed = (yf[slot, pl.ds(hint(k * t, 16), t), :] + sb[slot].astype(F32)).astype(BF16)
         zs[slot] = summed
         send(zs.at[slot], zr.at[bb, z], (r, 2 * zz + b), z_sems.at[bb, z], zz != z)
@@ -446,21 +478,45 @@
             zr[q, 0].astype(F32) + zr[q, 1].astype(F32) + zr[q, 2].astype(F32) + zr[q, 3].astype(F32)
         ).astype(BF16)
 
+    def d_w_down(source, part):
+        @pl.loop(0, half // u_tile)
+        def _(n):
+            units = pl.ds(hint(n * u_tile, 128), u_tile)
+            wd[part, units, :] = lax.dot_general(
+                source[0:tokens, units],
+                dout[:, pl.ds(hint(k * feat, 128), feat)],
+                (((0,), (0,)), ((), ())),
+                preferred_element_type=F32,
+            ).astype(BF16)
+
+        part_rows = pl.ds(hint(part * half, 16), half)
+        return fetch(wd.at[part], dw_hbm.at[part_rows, :])
+
     product(slot_own, 0)
     product(slot_own, 1)
+    arrived(hid_slot(slot_fo), hid_recv[7])
+    hid_to_sibling(slot_fo)
+    fetch(hid.at[:, own_half], wg.at[0:tokens]).wait()
+    own_dw = d_w_down(wg, k)
     for h in both:
         arrived(whole(slot_l, pieces[h]), dg_recv[1][h])
         send_same(one(slot_l, 0, pieces[h]), right, dg_recv[3][h])
+        send_same(rest(slot_l, pieces[h]), partner, dg_recv[8][h])
         arrived(whole(slot_r, pieces[h]), dg_recv[2][h])
         send_same(one(slot_r, 1, pieces[h]), left, dg_recv[4][h])
+        send_same(rest(slot_r, pieces[h]), partner, dg_recv[9][h])
         if h == 0:
             combine()
             product(slot_l, 0)
             product(slot_r, 0)
+            for slot, sem in hid_sib:
+                arrived(hid.at[pl.ds(hint(slot * 2 * t, 16), 2 * t), other_half], sem)
+            fetch(hid.at[:, other_half], wu.at[0:tokens]).wait()
+            other_dw = d_w_down(wu, k1)
     for h in both:
         arrived(whole(slot_part, pieces[h]), dg_recv[0][h])
-        send_same(whole(slot_part, pieces[h]), right, dg_recv[5][h])
-        send_same(whole(slot_part, pieces[h]), left, dg_recv[6][h])
+        send_same(most(slot_part, pieces[h]), right, dg_recv[5][h])
+        send_same(most(slot_part, pieces[h]), left, dg_recv[6][h])
     product(slot_l, 1)
     product(slot_r, 1)
     for h in both:
@@ -478,36 +534,28 @@
 
     same = lax.rem(y + b, 2)
     over_z(y)
-    send(vs.at[y], dn.at[same], perm_from(y), d_sems.at[same], off_diagonal)
-
-    @pl.when(diagonal)
+    send(vs.at[y], dn.at[same], sum_to(y), d_sems.at[same], not_own_sum)
+
+    @pl.when(own_sum)
     def _():
         dn[same] = vs[y]
-
-    arrived(hid_slot(slot_lo), hid_recv[5])
-    hid_to_sibling(slot_lo)
-    arrived(hid_slot(slot_ro), hid_recv[6])
-    hid_to_sibling(slot_ro)
-    arrived(hid_slot(slot_fo), hid_recv[7])
-    hid_to_sibling(slot_fo)
 
     for h in both:
         arrived(whole(slot_fo, pieces[h]), dg_recv[7][h])
         product(slot_fo, h)
-        arrived(whole(slot_lo, pieces[h]), dg_recv[5][h])
+        arrived(most(slot_lo, pieces[h]), dg_recv[5][h])
+        arrived(rest(slot_lo, pieces[h]), dg_recv[8][h])
         product(slot_lo, h)
-        arrived(whole(slot_ro, pieces[h]), dg_recv[6][h])
+        arrived(most(slot_ro, pieces[h]), dg_recv[6][h])
+        arrived(rest(slot_ro, pieces[h]), dg_recv[9][h])
         product(slot_ro, h)
     combine()
     combine()
     combine()
     over_z(y1)
-    send(vs.at[y1], dn.at[1 - same], perm_from(y1), d_sems.at[1 - same])
-
-    for slot, sem in hid_sib:
-        arrived(hid.at[slot, :, other_half], sem)
-
-    @pl.when(off_diagonal)
+    send(vs.at[y1], dn.at[1 - same], sum_to(y1), d_sems.at[1 - same])
+
+    @pl.when(not_own_sum)
     def _():
         arrived(dn.at[0], d_sems.at[0])
 
@@ -532,13 +580,18 @@
         outv[...].astype(F32) + inverse_mid_column * (scaled - normed * (inner_column / model))
     ).astype(BF16)
     final = fetch(outv, out_hbm)
-    dout_copy.wait()
+    own_dw.wait()
+    other_dw.wait()
     final.wait()
     for copy, when in sent:
         if when is None:
             copy.wait_send()
         else:
             pl.when(when)(copy.wait_send)
+
+
+def widen(narrow, wide):
+    wide[...] = narrow[...].astype(F32)
 
 
 def local(
@@ -549,12 +602,12 @@
     half, feat = units // 2, width // 2
     any_spec = pl.BlockSpec(memory_space=pl.ANY)
     vm = pltpu.VMEM
-    out, hid, dout = pl.pallas_call(
+    out, _, d_w_down = pl.pallas_call(
         kernel,
         out_shape=(
             jax.ShapeDtypeStruct((t, width), BF16),
-            jax.ShapeDtypeStruct((8, 2 * t, units), BF16),
-            jax.ShapeDtypeStruct((16 * t, feat), BF16),
+            jax.ShapeDtypeStruct((16 * t, units), BF16),
+            jax.ShapeDtypeStruct((units, feat), BF16),
         ),
         in_specs=[any_spec] * 12,
         out_specs=(any_spec,) * 3,
@@ -616,9 +669,15 @@
         final_gain.reshape(1, width), mlp_gain.reshape(1, width), value_weight.reshape(1, width),
         returns.reshape(1, t), response_mask.reshape(1, t), w_gate, w_up, w_down,
     )
-    d_w_down = lax.dot_general(
-        hid.reshape(16 * t, units), dout, (((0,), (0,)), ((), ())), preferred_element_type=F32
-    )
+    rows = units // 7 if units % (7 * 16) == 0 else units
+    spec = pl.BlockSpec((rows, feat), lambda i: (i, 0))
+    d_w_down = pl.pallas_call(
+        widen,
+        out_shape=jax.ShapeDtypeStruct((units, feat), F32),
+        grid=(units // rows,),
+        in_specs=[spec],
+        out_specs=spec,
+    )(d_w_down)
     return out, d_w_down
 
 

time: 136 us -> 133 us (0.978)
  matrix products: 8.89 us -> 0 us
  Pallas kernels: 124 us -> 130 us
    dot_general x1 -> x0, matrix products: 8.89 us -> none  [local(): lax.dot_general(hid.reshape(16 * t, units), dout, (((0,), (0,)), ((), ())...]
    pallas_call x0 -> x1, Pallas kernels: none -> 6.72 us  [local(): pl.pallas_call(widen, out_shape=jax.ShapeDtypeStruct((units, feat), F32),...]
where the time goes in v3:
time: 133 us; the launch traced here: 132 us
  Pallas kernels  130 us (98%)
    pallas_call x1, Pallas kernels, local(): pl.pallas_call(kernel, out_shape=(jax.ShapeDtypeStruct((t, width), BF16),...  124 us
    pallas_call x1, Pallas kernels, local(): pl.pallas_call(widen, out_shape=jax.ShapeDtypeStruct((units, feat), F32),...  6.72 us

profile of v3, /device:TPU:2, one launch (start us, length us, event | category | flops | bytes accessed | tf_op | source)
XLA Modules:
  0.0 131.6 jit_solution(15833438391569492834)
XLA Ops:
  0.6 123.6 %shard_map.131 = (bf16[48,1024]{1,0:T(8,128)(2,1)}, bf16[768,3584]{1,0:T(8,128)(2,1)}, bf16[3584,512]{1,0:T(8,128)(2,1)}) custom-call(bf16[48,1024]{1,0:T(8,128)(2,1)} %block_hbm.1, bf16[48,1024]{1,0:T(8,128)(2,1)} %mid_hbm.1, bf16[48,3584]{1,0:T(8,128)(2,1)} %gate_hbm.1, bf16[48,3584]{1,0:T(8,128)(2,1)} %up_hbm.1, f32[1,1024]{1,0:T(1,128)} %bitcast.5, ...), custom_call_target="tpu_custom_call" | custom-call | tf_op jit(solution)/shard_map/pallas_call | solution.py:605
  124.2 0.0 copy-start
  124.3 6.7 %shard_map.132 = f32[3584,512]{1,0:T(8,128)} custom-call(bf16[3584,512]{1,0:T(8,128)(2,1)} %get-tuple-element.5.narrow), custom_call_target="tpu_custom_call" | custom-call | tf_op jit(solution)/shard_map/pallas_call | solution.py:674
  131.0 0.0 copy-done
  131.0 0.6 copy.15
Async XLA Ops:
  124.2 6.7 %copy-start = (bf16[48,1024]{1,0:T(8,128)(2,1)S(1)}, bf16[48,1024]{1,0:T(8,128)(2,1)}, u32[]{:S(2)}) copy-start(bf16[48,1024]{1,0:T(8,128)(2,1)} %get-tuple-element.8) | copy-start | bytes 294916

commit v4 on v3

--- a/solution.py
+++ b/solution.py
@@ -281,18 +281,18 @@
     tile_to_sibling(2 * z + b1)
     arrived(tile.at[k, 2 * zp + b], t_own_p)
     tile_to_sibling(2 * zp + b)
-
-    arrived(tile.at[k, 2 * zp + b1], t_oth_p)
-    send_same(tile.at[k, 2 * zp + b1], z_minus, t_far_oth)
-    tile_to_sibling(2 * zp + b1)
-    arrived(tile.at[k, 2 * zm + b1], t_oth_m)
-    tile_to_sibling(2 * zm + b1)
     arrived(hid_slot(slot_l), hid_recv[1])
     send_same(hid_slot(slot_l, 0), right, hid_recv[3])
     send_same(hid_slot(slot_l, t), partner, hid_recv[8])
     arrived(hid_slot(slot_r), hid_recv[2])
     send_same(hid_slot(slot_r, t), left, hid_recv[4])
     send_same(hid_slot(slot_r, t), partner, hid_recv[9])
+
+    arrived(tile.at[k, 2 * zp + b1], t_oth_p)
+    send_same(tile.at[k, 2 * zp + b1], z_minus, t_far_oth)
+    tile_to_sibling(2 * zp + b1)
+    arrived(tile.at[k, 2 * zm + b1], t_oth_m)
+    tile_to_sibling(2 * zm + b1)
     arrived(tile.at[k, 2 * zf + b], t_far_own)
     tile_to_sibling(2 * zf + b)
 
@@ -351,6 +351,9 @@
         send(chunk(slot_ro, pieces[h]), nl.at[:, pieces[h]], right, nl_s[h])
         hidden(slot_lo, pieces[h])
         send(chunk(slot_lo, pieces[h]), nr.at[:, pieces[h]], left, nr_s[h])
+    arrived(hid_slot(slot_f, 0), hid_recv[3])
+    arrived(hid_slot(slot_f, t), hid_recv[4])
+    send_same(hid_slot(slot_f), partner, hid_recv[7])
     for h in both:
         hidden(slot_f, pieces[h])
         arrived(rf.at[:, pieces[h]], rf_s[h])
@@ -376,15 +379,13 @@
     for h in both:
         hidden(slot_own, pieces[h])
 
-    arrived(hid_slot(slot_f, 0), hid_recv[3])
-    arrived(hid_slot(slot_f, t), hid_recv[4])
-    send_same(hid_slot(slot_f), partner, hid_recv[7])
     own_hid.wait()
     arrived(hid_slot(slot_lo, 0), hid_recv[5])
     arrived(hid_slot(slot_ro, 0), hid_recv[6])
     arrived(hid_slot(slot_lo, t), hid_recv[8])
     arrived(hid_slot(slot_ro, t), hid_recv[9])
-    for slot in (slot_own, slot_l, slot_r, slot_part, slot_f, slot_lo, slot_ro):
+    arrived(hid_slot(slot_fo), hid_recv[7])
+    for slot in (slot_own, slot_l, slot_r, slot_part, slot_f, slot_lo, slot_ro, slot_fo):
         hid_to_sibling(slot)
     for copy in weights_in:
         copy.wait()
@@ -494,8 +495,6 @@
 
     product(slot_own, 0)
     product(slot_own, 1)
-    arrived(hid_slot(slot_fo), hid_recv[7])
-    hid_to_sibling(slot_fo)
     fetch(hid.at[:, own_half], wg.at[0:tokens]).wait()
     own_dw = d_w_down(wg, k)
     for h in both:
@@ -588,10 +587,6 @@
             copy.wait_send()
         else:
             pl.when(when)(copy.wait_send)
-
-
-def widen(narrow, wide):
-    wide[...] = narrow[...].astype(F32)
 
 
 def local(
@@ -669,16 +664,7 @@
         final_gain.reshape(1, width), mlp_gain.reshape(1, width), value_weight.reshape(1, width),
         returns.reshape(1, t), response_mask.reshape(1, t), w_gate, w_up, w_down,
     )
-    rows = units // 7 if units % (7 * 16) == 0 else units
-    spec = pl.BlockSpec((rows, feat), lambda i: (i, 0))
-    d_w_down = pl.pallas_call(
-        widen,
-        out_shape=jax.ShapeDtypeStruct((units, feat), F32),
-        grid=(units // rows,),
-        in_specs=[spec],
-        out_specs=spec,
-    )(d_w_down)
-    return out, d_w_down
+    return out, d_w_down.astype(F32)
 
 
 def solution(mesh):

time: 133 us -> 128 us (0.962)
  Pallas kernels: 130 us -> 120 us
  other arithmetic: 0 us -> 6.17 us
    pallas_call x1 -> x0, Pallas kernels: 6.72 us -> none  [local(): pl.pallas_call(widen, out_shape=jax.ShapeDtypeStruct((units, feat), F32),...]
    convert_element_type x0 -> x1, other arithmetic: none -> 6.17 us  [local(): return (out, d_w_down.astype(F32))]
    pallas_call x1, Pallas kernels: 124 us -> 120 us  [local(): pl.pallas_call(kernel, out_shape=(jax.ShapeDtypeStruct((t, width), BF16),...]
where the time goes in v4:
time: 128 us
  Pallas kernels  120 us (94%)
  other arithmetic  6.17 us (5%)
    pallas_call x1, Pallas kernels, local(): pl.pallas_call(kernel, out_shape=(jax.ShapeDtypeStruct((t, width), BF16),...  120 us
    convert_element_type x1, other arithmetic, local(): return (out, d_w_down.astype(F32))  6.17 us

profile of v4, /device:TPU:2, one launch (start us, length us, event | category | flops | bytes accessed | tf_op | source)
XLA Modules:
  0.0 127.7 jit_solution(8575016549202325523)
XLA Ops:
  0.6 120.2 %shard_map.131 = (bf16[48,1024]{1,0:T(8,128)(2,1)}, bf16[768,3584]{1,0:T(8,128)(2,1)}, bf16[3584,512]{1,0:T(8,128)(2,1)}) custom-call(bf16[48,1024]{1,0:T(8,128)(2,1)} %block_hbm.1, bf16[48,1024]{1,0:T(8,128)(2,1)} %mid_hbm.1, bf16[48,3584]{1,0:T(8,128)(2,1)} %gate_hbm.1, bf16[48,3584]{1,0:T(8,128)(2,1)} %up_hbm.1, f32[1,1024]{1,0:T(1,128)} %bitcast.5, ...), custom_call_target="tpu_custom_call" | custom-call | tf_op jit(solution)/shard_map/pallas_call | solution.py:600
  120.9 0.0 copy-start
  120.9 6.2 %convert_element_type.3 = f32[3584,512]{1,0:T(8,128)} convert(bf16[3584,512]{1,0:T(8,128)(2,1)} %get-tuple-element.5) | non-fusion elementwise | flops 1835008 | bytes 11010048 | tf_op jit(solution)/shard_map/convert_element_type | solution.py:667
  127.0 0.0 copy-done
  127.0 0.6 copy.15
Async XLA Ops:
  120.9 6.2 %copy-start = (bf16[48,1024]{1,0:T(8,128)(2,1)S(1)}, bf16[48,1024]{1,0:T(8,128)(2,1)}, u32[]{:S(2)}) copy-start(bf16[48,1024]{1,0:T(8,128)(2,1)} %get-tuple-element.8) | copy-start | bytes 294916

commit v5 on v4

--- a/solution.py
+++ b/solution.py
@@ -219,8 +219,6 @@
         send_same(hid_slot(slot), sibling, hid_sib[-1][1])
 
     own_hid = fetch(hid_own, hid_slot(slot_own))
-    send(hid_own, hid_slot(slot_own), right, hid_recv[1])
-    send(hid_own, hid_slot(slot_own), left, hid_recv[2])
 
     for step in (1, 7, 2, 6, 3, 5, 4):
         arrived(stat.at[lax.rem(c + 8 - step, 8)], stat_recv[step])
@@ -260,6 +258,8 @@
     send_same(tile.at[k, c], z_plus, t_own_m)
     send_same(tile.at[k, c], z_minus, t_own_p)
     tile_to_sibling(c)
+    send(hid_own, hid_slot(slot_own), right, hid_recv[1])
+    send(hid_own, hid_slot(slot_own), left, hid_recv[2])
     send(hid_own, hid_slot(slot_own), partner, hid_recv[0])
 
     weights_down.wait()
@@ -281,16 +281,16 @@
     tile_to_sibling(2 * z + b1)
     arrived(tile.at[k, 2 * zp + b], t_own_p)
     tile_to_sibling(2 * zp + b)
+
+    arrived(tile.at[k, 2 * zp + b1], t_oth_p)
+    send_same(tile.at[k, 2 * zp + b1], z_minus, t_far_oth)
+    tile_to_sibling(2 * zp + b1)
     arrived(hid_slot(slot_l), hid_recv[1])
     send_same(hid_slot(slot_l, 0), right, hid_recv[3])
     send_same(hid_slot(slot_l, t), partner, hid_recv[8])
     arrived(hid_slot(slot_r), hid_recv[2])
     send_same(hid_slot(slot_r, t), left, hid_recv[4])
     send_same(hid_slot(slot_r, t), partner, hid_recv[9])
-
-    arrived(tile.at[k, 2 * zp + b1], t_oth_p)
-    send_same(tile.at[k, 2 * zp + b1], z_minus, t_far_oth)
-    tile_to_sibling(2 * zp + b1)
     arrived(tile.at[k, 2 * zm + b1], t_oth_m)
     tile_to_sibling(2 * zm + b1)
     arrived(tile.at[k, 2 * zf + b], t_far_own)
@@ -545,10 +545,11 @@
         arrived(most(slot_lo, pieces[h]), dg_recv[5][h])
         arrived(rest(slot_lo, pieces[h]), dg_recv[8][h])
         product(slot_lo, h)
+        if h == 1:
+            combine()
         arrived(most(slot_ro, pieces[h]), dg_recv[6][h])
         arrived(rest(slot_ro, pieces[h]), dg_recv[9][h])
         product(slot_ro, h)
-    combine()
     combine()
     combine()
     over_z(y1)

time: 128 us -> 129 us (level)
  no operation moved by 1% of the time
where the time goes in v5:
time: 129 us; the launch traced here: 128 us
  Pallas kernels  120 us (93%)
  other arithmetic  6.17 us (5%)
    pallas_call x1, Pallas kernels, local(): pl.pallas_call(kernel, out_shape=(jax.ShapeDtypeStruct((t, width), BF16),...  120 us
    convert_element_type x1, other arithmetic, local(): return (out, d_w_down.astype(F32))  6.17 us

profile of v5, /device:TPU:2, one launch (start us, length us, event | category | flops | bytes accessed | tf_op | source)
XLA Modules:
  0.0 127.6 jit_solution(11053150065636053915)
XLA Ops:
  0.6 120.1 %shard_map.131 = (bf16[48,1024]{1,0:T(8,128)(2,1)}, bf16[768,3584]{1,0:T(8,128)(2,1)}, bf16[3584,512]{1,0:T(8,128)(2,1)}) custom-call(bf16[48,1024]{1,0:T(8,128)(2,1)} %block_hbm.1, bf16[48,1024]{1,0:T(8,128)(2,1)} %mid_hbm.1, bf16[48,3584]{1,0:T(8,128)(2,1)} %gate_hbm.1, bf16[48,3584]{1,0:T(8,128)(2,1)} %up_hbm.1, f32[1,1024]{1,0:T(1,128)} %bitcast.5, ...), custom_call_target="tpu_custom_call" | custom-call | tf_op jit(solution)/shard_map/pallas_call | solution.py:601
  120.8 0.0 copy-start
  120.8 6.2 %convert_element_type.3 = f32[3584,512]{1,0:T(8,128)} convert(bf16[3584,512]{1,0:T(8,128)(2,1)} %get-tuple-element.5) | non-fusion elementwise | flops 1835008 | bytes 11010048 | tf_op jit(solution)/shard_map/convert_element_type | solution.py:668
  127.0 0.0 copy-done
  127.0 0.6 copy.15
Async XLA Ops:
  120.8 6.2 %copy-start = (bf16[48,1024]{1,0:T(8,128)(2,1)S(1)}, bf16[48,1024]{1,0:T(8,128)(2,1)}, u32[]{:S(2)}) copy-start(bf16[48,1024]{1,0:T(8,128)(2,1)} %get-tuple-element.8) | copy-start | bytes 294916
